TPU v7x, 512 devices: a whole 4x4x16 slice. The times are simulated.
512 devices in a mesh: theta: 64 (over z, y_hi, core), gz: 8 (over x, y_lo).
Axes of the slice: x: 4, y: 4 (y_hi: 2, y_lo: 2; y = y_hi * 2 + y_lo), z: 16, core: 2. Of those that a mesh axis runs over, the one named last changes fastest.
Arguments:
- fluid_state: float32 [8, 64, 1024, 128], P(None, 'gz', 'theta'), may hold values from -5 to 20, as said below
- levels: int32 [4, 128], P(None, 'theta'), may hold values from 0 to 1, as said below
- fine_rim: float32 [512, 2, 8, 1024], P('theta', None, None, 'gz'), may hold values from -1.5 to 3, as said below
- slot_owner: int32 [512], replicated, may hold values from 0 to 63, as said below
- slot_block: int32 [512], replicated, may hold values from 0 to 1
- slot_count: int32 [64], replicated, may hold values from 0 to 8, as said below
Outputs:
- residual: float32 [8, 64, 1024, 128], P(None, 'gz', 'theta')
- flux_mismatch: float32 [8, 64, 1024], P(None, 'gz', 'theta')
- inner_flux: float32 [8, 64, 1024], P(None, 'gz', 'theta')
Inputs may be any that keep to these rules, and one draw needn't show every extreme that they name: `fluid_state`: density and pressure are positive; velocities and fields up to 1.5 in magnitude. `fine_rim`: primitive variables: density and pressure positive, velocity and field components up to 1.5 in magnitude. `levels`: each column is 1 on its first r blocks and 0 after, with at least one 1 and one 0. `slot_owner`: slot d * 8 + s belongs to theta device d; the valid slots of a device are its first slot_count[d]; values of other slots are arbitrary; every pair of owner and block is named by exactly two valid slots. `slot_count`: some device fills all 8 slots in every draw.
All inputs are finite; a program needn't handle non-finite values.
Results may differ from a plain program's by a relative error of at most 0.0003.
Values sent between devices are 32-bit elements; how exact they have to be, the bound alone decides.
A program may use at most 64 MiB of HBM per device.

v0:
```python
import math

import jax
import jax.numpy as jnp
from jax import lax
from jax.sharding import PartitionSpec as P

BT = 8
BR = 32


GAMMA = 5.0 / 3.0
AXIS_FLIP = (1.0, -1.0, -1.0, 1.0, 1.0, -1.0, -1.0, 1.0)


def extended_2(cells, sides, width, closed):
    for axis, dim in sides:
        count = lax.axis_size(axis)
        ends = count if closed else count - 1
        head = lax.slice_in_dim(cells, 0, width, axis=dim)
        tail = lax.slice_in_dim(cells, cells.shape[dim] - width, cells.shape[dim], axis=dim)
        cells = jnp.concatenate(
            [
                lax.ppermute(tail, axis, [(i, (i + 1) % count) for i in range(ends)]),
                cells,
                lax.ppermute(head, axis, [((i + 1) % count, i) for i in range(ends)]),
            ],
            axis=dim,
        )
    return cells


def from_partner(block, axis, distance):
    count = lax.axis_size(axis)
    route = []
    for low in range(count):
        high = low | 1 << distance
        if high != low and high < count:
            route += [(low, high), (high, low)]
    return lax.ppermute(block, axis, route)


def primitive(conserved):
    density = conserved[0]
    vel_r = conserved[1] / density
    vel_t = conserved[2] / density
    vel_z = conserved[3] / density
    kinetic = 0.5 * density * (vel_r * vel_r + vel_t * vel_t + vel_z * vel_z)
    magnetic = 0.5 * (
        conserved[5] * conserved[5] + conserved[6] * conserved[6] + conserved[7] * conserved[7]
    )
    pressure = (GAMMA - 1.0) * (conserved[4] - kinetic - magnetic)
    return jnp.stack(
        [density, vel_r, vel_t, vel_z, pressure, conserved[5], conserved[6], conserved[7]]
    )


def physical(states, normal):
    density = states[0]
    velocity = (states[1], states[2], states[3])
    pressure = states[4]
    field = (states[5], states[6], states[7])
    vel_n = velocity[normal]
    field_n = field[normal]
    field_sq = field[0] * field[0] + field[1] * field[1] + field[2] * field[2]
    speed_sq = velocity[0] * velocity[0] + velocity[1] * velocity[1] + velocity[2] * velocity[2]
    vel_dot = velocity[0] * field[0] + velocity[1] * field[1] + velocity[2] * field[2]
    total_p = pressure + 0.5 * field_sq
    energy = pressure / (GAMMA - 1.0) + 0.5 * density * speed_sq + 0.5 * field_sq
    conserved = jnp.stack(
        [
            density,
            density * velocity[0],
            density * velocity[1],
            density * velocity[2],
            energy,
            field[0],
            field[1],
            field[2],
        ]
    )
    momentum = [
        density * velocity[component] * vel_n
        - field[component] * field_n
        + (total_p if component == normal else 0.0)
        for component in (0, 1, 2)
    ]
    induction = [
        vel_n * field[component] - field_n * velocity[component] for component in (0, 1, 2)
    ]
    fluxes = jnp.stack(
        [density * vel_n] + momentum + [(energy + total_p) * vel_n - field_n * vel_dot] + induction
    )
    signal = jnp.abs(vel_n) + jnp.sqrt((GAMMA * pressure + field_sq) / density)
    return (conserved, fluxes, signal)


def rusanov(left_state, right_state, normal):
    cons_left, flux_left, signal_left = physical(left_state, normal)
    cons_right, flux_right, signal_right = physical(right_state, normal)
    return 0.5 * (flux_left + flux_right) - 0.5 * jnp.maximum(signal_left, signal_right) * (
        cons_right - cons_left
    )


def minmod(lower_diff, upper_diff):
    return (
        0.5
        * (jnp.sign(lower_diff) + jnp.sign(upper_diff))
        * jnp.minimum(jnp.abs(lower_diff), jnp.abs(upper_diff))
    )


def face_pairs(extended, axis_dim, length):
    middle = lax.slice_in_dim(extended, 1, length + 3, axis=axis_dim)
    behind = lax.slice_in_dim(extended, 0, length + 2, axis=axis_dim)
    beyond = lax.slice_in_dim(extended, 2, length + 4, axis=axis_dim)
    slopes = minmod(middle - behind, beyond - middle)
    left_state = lax.slice_in_dim(middle + 0.5 * slopes, 0, length + 1, axis=axis_dim)
    right_state = lax.slice_in_dim(middle - 0.5 * slopes, 1, length + 2, axis=axis_dim)
    return (left_state, right_state)


def local_residual(conserved, theta_ext, axial_ext, partner_row, dtheta):
    fields, depth_z, width_t, radial = conserved.shape
    states = primitive(conserved)
    theta_states = jnp.concatenate(
        [primitive(theta_ext[:, :, :2]), states, primitive(theta_ext[:, :, -2:])], axis=2
    )
    axial_states = jnp.concatenate(
        [primitive(axial_ext[:, :2]), states, primitive(axial_ext[:, -2:])], axis=1
    )
    flipper = jnp.array(AXIS_FLIP, jnp.float32).reshape(-1, 1, 1)
    across = primitive(partner_row) * flipper
    behind = jnp.concatenate([across[..., None], states[..., :-1]], axis=-1)
    beyond = jnp.concatenate([states[..., 1:], states[..., -1:]], axis=-1)
    slopes = minmod(states - behind, beyond - states)
    left_state = states + 0.5 * slopes
    right_state = jnp.concatenate([(states - 0.5 * slopes)[..., 1:], states[..., -1:]], axis=-1)
    radial_flux = rusanov(left_state, right_state, 0)
    face_radius = jnp.arange(radial, dtype=jnp.float32) + 1.0
    cell_radius = jnp.arange(radial, dtype=jnp.float32) + 0.5
    outward = radial_flux * (face_radius * dtheta)
    inward = jnp.concatenate([jnp.zeros_like(outward[..., :1]), outward[..., :-1]], axis=-1)
    theta_left, theta_right = face_pairs(theta_states, 2, width_t)
    theta_flux = rusanov(theta_left, theta_right, 1)
    axial_left, axial_right = face_pairs(axial_states, 1, depth_z)
    axial_flux = rusanov(axial_left, axial_right, 2)
    residual = (
        inward
        - outward
        - (theta_flux[:, :, 1:] - theta_flux[:, :, :-1])
        - (axial_flux[:, 1:] - axial_flux[:, :-1]) * (cell_radius * dtheta)
    )
    density = states[0]
    vel_r = states[1]
    vel_t = states[2]
    pressure = states[4]
    field_r = states[5]
    field_t = states[6]
    field_sq = states[5] * states[5] + states[6] * states[6] + states[7] * states[7]
    residual = residual.at[1].add(
        dtheta * (density * vel_t * vel_t + pressure + 0.5 * field_sq - field_t * field_t)
    )
    residual = residual.at[2].add(-dtheta * (density * vel_r * vel_t - field_r * field_t))
    residual = residual.at[6].add(dtheta * (vel_r * field_t - vel_t * field_r))
    return (residual, radial_flux)


def reflux(residual, radial_flux, fine_cells, face_index, dtheta):
    radial = residual.shape[-1]
    positions = jnp.arange(radial, dtype=jnp.int32)
    pick_face = (positions[None, :] == (face_index - 1)[:, None]).astype(jnp.float32)
    coarse_face = jnp.sum(radial_flux * pick_face, axis=-1)
    mismatch = fine_cells - coarse_face
    area = face_index.astype(jnp.float32) * dtheta
    correction = area * mismatch
    outer_cell = (positions[None, :] == face_index[:, None]).astype(jnp.float32)
    volume = (jnp.arange(radial, dtype=jnp.float32) + 0.5) * dtheta
    return ((residual + correction[..., None] * outer_cell) / volume, mismatch)


def fine_faces(fine_rim):
    rim_states = jnp.moveaxis(fine_rim, 2, 0)
    flux_out = rusanov(rim_states[:, :, 0], rim_states[:, :, 1], 0)
    fields, slot_total, length = flux_out.shape
    paired = flux_out.reshape(fields, slot_total, length // (2 * BT), BT, 2)
    return 0.25 * jnp.sum(paired, axis=-1)


def body(fluid_state, levels, fine_rim, slot_owner, slot_block, slot_count):
    fields, depth_z, width_t, radial = fluid_state.shape
    devices = lax.axis_size("theta")
    dtheta = 2.0 * math.pi / (width_t * devices)
    theta_pos = lax.axis_index("theta")
    theta_ext = extended_2(fluid_state, (("theta", 2),), 2, True)
    axial_raw = extended_2(fluid_state, (("gz", 1),), 2, False)
    axial_pos = lax.axis_index("gz")
    ghost_shape = (fields, 2, width_t, radial)
    bottom = jnp.where(
        axial_pos == 0, jnp.broadcast_to(fluid_state[:, :1], ghost_shape), axial_raw[:, :2]
    )
    upper_ghost = jnp.where(
        axial_pos == lax.axis_size("gz") - 1,
        jnp.broadcast_to(fluid_state[:, -1:], ghost_shape),
        axial_raw[:, -2:],
    )
    axial_ext = jnp.concatenate([bottom, fluid_state, upper_ghost], axis=1)
    first_row = fluid_state[..., 0].reshape(fields, depth_z * width_t)
    across = from_partner(first_row, "theta", devices.bit_length() - 2)
    partner_row = across.reshape(fields, depth_z, width_t)
    residual, radial_flux = local_residual(fluid_state, theta_ext, axial_ext, partner_row, dtheta)
    partials = fine_faces(fine_rim)
    slot_cap = fine_rim.shape[0]
    live_slots = (jnp.arange(slot_cap, dtype=jnp.int32) < slot_count[theta_pos]).astype(jnp.float32)
    partials = partials * live_slots[None, :, None, None]
    rows_out = jnp.moveaxis(partials, 1, 0).reshape(slot_cap, fields * depth_z * BT)
    blocks_dev = width_t // BT
    chosen = (
        (slot_owner == theta_pos)[None, :]
        & (slot_block[None, :] == jnp.arange(blocks_dev, dtype=jnp.int32)[:, None])
    ).astype(jnp.float32)
    registers = jnp.dot(
        chosen,
        lax.all_gather(rows_out, "theta", axis=0, tiled=True),
        precision=lax.Precision.HIGHEST,
    )
    fine_cells = (
        registers.reshape(blocks_dev, fields, depth_z, BT)
        .transpose(1, 2, 0, 3)
        .reshape(fields, depth_z, width_t)
    )
    face_index = jnp.repeat(BR * jnp.sum(levels, axis=0), BT)
    result, mismatch = reflux(residual, radial_flux, fine_cells, face_index, dtheta)
    return (result, mismatch, radial_flux[..., 0])


def solution(mesh):
    return jax.shard_map(
        body,
        mesh=mesh,
        in_specs=(
            P(None, "gz", "theta", None),
            P(None, "theta"),
            P("theta", None, None, "gz"),
            P(),
            P(),
            P(),
        ),
        out_specs=(P(None, "gz", "theta", None), P(None, "gz", "theta"), P(None, "gz", "theta")),
        check_vma=False,
    )
```

profile of v0, /device:TPU:1, one launch (start us, length us, event | category | flops | bytes accessed | tf_op | source)
XLA Modules:
  0.0 194.4 jit_solution(17062907998773435416)
XLA Ops:
  7.2 1.7 fusion.64
  9.0 1.3 collective-permute-start.4
  10.2 5.3 %collective-permute-start.3 = (f32[8,2,16,128]{3,2,1,0:T(8,128)}, f32[8,2,16,128]{3,2,1,0:T(8,128)}, u32[]{:S(2)}, u32[]{:S(2)}) collective-permute-start(f32[8,2,16,128]{3,2,1,0:T(8,128)} %get-tuple-element.146), channel_id=1, source_target_pairs={{0,1},{1,2},{2,3},{3,4},{4,5},{5,6},{6,7},{8,9},{9,10},{10,11},{11... | collective-permute-start | bytes 393224 | tf_op jit(solution)/shard_map/ppermute | solution.py:24
  15.6 0.6 copy.490
  16.2 8.7 %collective-permute-start.2 = (f32[8,8,2,128]{3,1,2,0:T(8,128)}, f32[8,8,2,128]{3,1,2,0:T(8,128)S(1)}, u32[]{:S(2)}, u32[]{:S(2)}) collective-permute-start(f32[8,8,2,128]{3,1,2,0:T(8,128)} %copy.490), channel_id=1, source_target_pairs={{8,0},{16,8},{24,16},{32,24},{40,32},{48,40},{56,48},{64,56},{72,6... | collective-permute-start | bytes 196616 | tf_op jit(solution)/shard_map/ppermute | solution.py:26
  24.9 0.6 copy.489
  25.6 1.9 collective-permute-start.1
  27.5 0.2 slice_reduce_fusion.1
  27.8 12.9 %collective-permute-start = (f32[8,128]{1,0:T(8,128)S(1)}, f32[8,128]{1,0:T(8,128)S(1)}, u32[]{:S(2)}, u32[]{:S(2)}) collective-permute-start(f32[8,128]{1,0:T(8,128)S(1)} %reshape_squeeze.3), channel_id=1, source_target_pairs={{0,256},{256,0},{8,264},{264,8},{16,272},{272,16},{24,280},{280,24... | collective-permute-start | bytes 12296 | tf_op jit(solution)/shard_map/ppermute | solution.py:40
  44.8 0.2 subtract_reduce_fusion
  45.0 0.1 copy.488
  45.1 0.6 copy-done.11
  45.8 0.6 dynamic_slice.3
  46.4 0.6 compare_select_fusion
  47.0 0.7 copy.487
  47.8 0.6 add_multiply_fusion.6
  48.9 0.5 convert_multiply_fusion
  49.5 0.7 constant_dynamic-update-slice_fusion.1
  50.2 1.0 fusion.62
  51.2 0.5 broadcast_compare_fusion
  51.8 0.5 add_multiply_fusion.5
  52.3 0.2 copy.362
  52.4 0.2 slice.777
  52.7 0.5 broadcast.594
  53.2 0.7 slice_reduce_fusion.2
  54.6 0.6 copy-done.10
  55.2 0.7 broadcast_multiply_fusion.2
  55.9 1.2 copy.359
  57.1 1.6 fusion.61
  58.7 0.3 slice_subtract_fusion.2
  59.1 0.2 multiply_bitcast_fusion.2
  59.6 0.1 constant_dynamic-update-slice_fusion.30
  60.1 0.3 multiply_reduce_fusion
  60.4 0.7 copy-done.4
  61.1 0.8 slice_reduce_fusion
  62.1 0.3 fusion.4
  63.2 0.4 fusion.1
  63.6 0.9 broadcast_select_fusion
  64.7 0.4 fusion.3
  65.9 0.2 multiply_subtract_fusion
  66.1 0.6 copy-done.5
  66.7 0.3 fusion.7
  66.9 0.6 copy-done.1
  67.7 115.7 %all-gather.2.cloned.1.call-done = f32[512,512]{1,0:T(8,128)} async-done(((f32[8,512]{1,0:T(8,128)}), f32[512,512]{1,0:T(8,128)}) %all-gather.2.cloned.1.call-update) | async-done | bytes 1048592 | tf_op jit(solution)/shard_map/all_gather | solution.py:225
  183.4 1.7 fusion.47
  185.3 0.6 copy-done.9
  186.0 0.6 broadcast_multiply_fusion.3
  186.6 1.0 add_divide_fusion
  (207 shorter events, 7.8 us)
Async XLA Ops:
  7.2 8.4 %copy-start = (f32[8,8,16,128]{3,2,1,0:T(8,128)S(1)}, f32[8,8,16,128]{3,2,1,0:T(8,128)}, u32[]{:S(2)}) copy-start(f32[8,8,16,128]{3,2,1,0:T(8,128)} %param.13) | copy-start | bytes 1572868
  7.2 176.2 %all-gather.2.cloned.1.call-start = ((), (), s32[]{:S(2)}) async-start(), calls=%async_computation | async-start | bytes 1064960 | tf_op jit(solution)/shard_map/all_gather | solution.py:225
  9.0 54.6 %collective-permute-start.4 = (f32[8,2,16,128]{3,2,1,0:T(8,128)}, f32[8,2,16,128]{3,2,1,0:T(8,128)}, u32[]{:S(2)}, u32[]{:S(2)}) collective-permute-start(f32[8,2,16,128]{3,2,1,0:T(8,128)} %get-tuple-element.147), channel_id=1, source_target_pairs={{1,0},{2,1},{3,2},{4,3},{5,4},{6,5},{7,6},{9,8},{10,9},{11,10},{12... | collective-permute-start | bytes 393224 | tf_op jit(solution)/shard_map/ppermute | solution.py:26
  10.2 54.3 %collective-permute-start.3 = (f32[8,2,16,128]{3,2,1,0:T(8,128)}, f32[8,2,16,128]{3,2,1,0:T(8,128)}, u32[]{:S(2)}, u32[]{:S(2)}) collective-permute-start(f32[8,2,16,128]{3,2,1,0:T(8,128)} %get-tuple-element.146), channel_id=1, source_target_pairs={{0,1},{1,2},{2,3},{3,4},{4,5},{5,6},{6,7},{8,9},{9,10},{10,11},{11... | collective-permute-start | bytes 393224 | tf_op jit(solution)/shard_map/ppermute | solution.py:24
  16.2 45.7 %collective-permute-start.2 = (f32[8,8,2,128]{3,1,2,0:T(8,128)}, f32[8,8,2,128]{3,1,2,0:T(8,128)S(1)}, u32[]{:S(2)}, u32[]{:S(2)}) collective-permute-start(f32[8,8,2,128]{3,1,2,0:T(8,128)} %copy.490), channel_id=1, source_target_pairs={{8,0},{16,8},{24,16},{32,24},{40,32},{48,40},{56,48},{64,56},{72,6... | collective-permute-start | bytes 196616 | tf_op jit(solution)/shard_map/ppermute | solution.py:26
  25.6 36.4 %collective-permute-start.1 = (f32[8,8,2,128]{3,1,2,0:T(8,128)}, f32[8,8,2,128]{3,1,2,0:T(8,128)S(1)}, u32[]{:S(2)}, u32[]{:S(2)}) collective-permute-start(f32[8,8,2,128]{3,1,2,0:T(8,128)} %copy.489), channel_id=1, source_target_pairs={{0,8},{8,16},{16,24},{24,32},{32,40},{40,48},{48,56},{56,64},{64,7... | collective-permute-start | bytes 196616 | tf_op jit(solution)/shard_map/ppermute | solution.py:24
  27.5 13.2 %copy-start.2 = (f32[8,2,8,128]{3,2,1,0:T(8,128)S(1)}, f32[8,2,8,128]{3,2,1,0:T(8,128)}, u32[]{:S(2)}) copy-start(f32[8,2,8,128]{3,2,1,0:T(8,128)} %param.15) | copy-start | bytes 196612
  27.8 24.9 %collective-permute-start = (f32[8,128]{1,0:T(8,128)S(1)}, f32[8,128]{1,0:T(8,128)S(1)}, u32[]{:S(2)}, u32[]{:S(2)}) collective-permute-start(f32[8,128]{1,0:T(8,128)S(1)} %reshape_squeeze.3), channel_id=1, source_target_pairs={{0,256},{256,0},{8,264},{264,8},{16,272},{272,16},{24,280},{280,24... | collective-permute-start | bytes 12296 | tf_op jit(solution)/shard_map/ppermute | solution.py:40
  45.1 0.7 copy-start.11
  47.8 0.7 copy-start.8
  50.2 1.0 copy-start.7
  54.6 0.7 copy-start.10
  60.4 0.7 copy-start.4
  66.1 0.6 copy-start.5
  66.7 0.8 copy-start.1
  67.6 115.8 %copy-start.3 = (s32[512]{0:T(512)S(1)}, s32[512]{0:T(512)}, u32[]{:S(2)}) copy-start(s32[512]{0:T(512)} %param.17) | copy-start | bytes 6148
  67.6 115.8 %copy-start.6 = (pred[512]{0:T(512)(128)(4,1)S(1)}, pred[512]{0:T(512)(128)(4,1)}, u32[]{:S(2)}) copy-start(pred[512]{0:T(512)(128)(4,1)} %broadcast_compare_fusion) | copy-start | bytes 1540
  185.3 0.6 copy-start.9
Sparse Core Ops, SparseCore 0:
  47.9 135.4 all-gather.1
where the time goes:
time: 195 us; the launch traced here: 194 us
  waiting for transfers between devices  116 us (59%)
  starting transfers between devices  30.1 us (15%)
  local copies, waits for them, and re-layouts  17.2 us (9%)
  between operations  15.3 us (8%)
  other arithmetic  14.4 us (7%)
    all_gather x1, waiting for transfers between devices, body(): lax.all_gather(rows_out, 'theta', axis=0, tiled=True)  116 us
    ppermute x1, starting transfers between devices, from_partner(): return lax.ppermute(block, axis, route)  12.9 us
    ppermute x2, starting transfers between devices, extended_2(): lax.ppermute(head, axis, [((i + 1) % count, i) for i in range(ends)])  9.94 us
    ppermute x2, starting transfers between devices, extended_2(): lax.ppermute(tail, axis, [(i, (i + 1) % count) for i in range(ends)])  7.23 us
    unnamed x45, local copies, waits for them, and re-layouts  5.39 us
  transfers between devices with their start and end apart: 6, of which 1 were waited for; matrix products, arithmetic and copies ran while one was open for 12% of the time, Pallas kernels for 0%

commit v1 on v0

v1 whole, which is shorter than its diff:
```python
import functools
import math

import jax
import jax.numpy as jnp
from jax import lax
from jax.experimental import pallas as pl
from jax.experimental.pallas import tpu as pltpu
from jax.sharding import PartitionSpec as P

BT = 8
BR = 32
GAMMA = 5.0 / 3.0
FLIPPED = (1, 2, 5, 6)
QUAD = 4
F32 = jnp.float32
MESH = pl.DeviceIdType.MESH


def primitive(cons):
    rho, mr, mt, mz, energy, br, bt, bz = cons
    inv = 1.0 / rho
    vr, vt, vz = mr * inv, mt * inv, mz * inv
    kinetic = mr * vr + mt * vt + mz * vz
    magnetic = br * br + bt * bt + bz * bz
    pressure = (GAMMA - 1.0) * (energy - 0.5 * (kinetic + magnetic))
    return [rho, vr, vt, vz, pressure, br, bt, bz]


def side_state(state, normal):
    rho, pressure = state[0], state[4]
    vel, field = state[1:4], state[5:8]
    mom = [rho * v for v in vel]
    vel_n, field_n = vel[normal], field[normal]
    field_sq = field[0] * field[0] + field[1] * field[1] + field[2] * field[2]
    half_sq = 0.5 * field_sq
    kinetic = 0.5 * (mom[0] * vel[0] + mom[1] * vel[1] + mom[2] * vel[2])
    vel_dot = vel[0] * field[0] + vel[1] * field[1] + vel[2] * field[2]
    total_p = pressure + half_sq
    energy = pressure * (1.0 / (GAMMA - 1.0)) + kinetic + half_sq
    flux = [mom[normal]]
    for comp in range(3):
        term = mom[comp] * vel_n - field[comp] * field_n
        flux.append(term + total_p if comp == normal else term)
    flux.append((energy + total_p) * vel_n - field_n * vel_dot)
    for comp in range(3):
        flux.append(None if comp == normal else vel_n * field[comp] - field_n * vel[comp])
    fast = GAMMA * pressure + field_sq
    signal = jnp.abs(vel_n) + fast * lax.rsqrt(fast * rho)
    return [rho] + mom + [energy] + list(field), flux, signal


def double_flux(left, right, normal):
    cons_l, flux_l, signal_l = side_state(left, normal)
    cons_r, flux_r, signal_r = side_state(right, normal)
    top = jnp.maximum(signal_l, signal_r)
    out = []
    for ul, ur, fl, fr in zip(cons_l, cons_r, flux_l, flux_r):
        if fl is None:
            out.append(top * (ul - ur))
        else:
            out.append((fl + fr) - top * (ur - ul))
    return out


def half_slope(lower, upper):
    low, high = jnp.minimum(lower, upper), jnp.maximum(lower, upper)
    return 0.5 * (jnp.maximum(low, 0.0) + jnp.minimum(high, 0.0))


def kernel(
    sizes,
    x_hbm, fine_hbm, levels_hbm, owner_hbm, block_hbm, count_hbm,
    res_ref, mis_ref, inner_ref,
    x_v, fine_v, prim_v, cross_v, edge_v, edge_in, packed_v, turned_v, corr_v,
    quad_v, out_v, in_v,
    levels_s, owner_s, block_s, count_s,
    load_sem, quad_send, quad_recv, ring_send, ring_recv, halo_send, halo_recv,
):
    theta_n, gz_n, depth, width, dtheta = sizes
    rows = depth * width
    ring_n = theta_n // QUAD
    theta = lax.axis_index("theta")
    gz = lax.axis_index("gz")
    ring_pos, quad_pos = theta // QUAD, theta % QUAD

    def load(src, dst, sem):
        return pltpu.make_async_copy(src, dst, load_sem.at[sem])

    loads = [
        load(fine_hbm, fine_v, 0),
        load(x_hbm, x_v, 1),
        load(levels_hbm, levels_s, 2),
        load(owner_hbm, owner_s, 3),
        load(block_hbm, block_s, 4),
        load(count_hbm, count_s, 5),
    ]
    for item in loads:
        item.start()

    barrier = pltpu.get_barrier_semaphore()
    greeted = 0

    def greet(t, g):
        pl.semaphore_signal(barrier, inc=1, device_id={"theta": t, "gz": g}, device_id_type=MESH)

    ring_steps = sorted(range(1, ring_n), key=lambda d: -min(d, ring_n - d))
    for step in ring_steps:
        greet((ring_pos + step) % ring_n * QUAD + quad_pos, gz)
        greeted += 1
    for t, g in (
        ((theta + 1) % theta_n, gz),
        ((theta + theta_n - 1) % theta_n, gz),
        (theta, (gz + 1) % gz_n),
        (theta, (gz + gz_n - 1) % gz_n),
    ):
        greet(t, g)
        greeted += 1
    for step in range(1, QUAD):
        greet(ring_pos * QUAD + (quad_pos + step) % QUAD, gz)
        greeted += 1

    lane = lax.broadcasted_iota(jnp.int32, (8, 128), 1)
    lane_block = (lane % width) // BT

    loads[0].wait()
    sides = [
        [fine_v[pl.ds(side * 8 + var, 8, stride=16), :] for var in range(8)] for side in (0, 1)
    ]
    fine_flux = jnp.concatenate(double_flux(sides[0], sides[1], 0), axis=0)
    src = lax.broadcasted_iota(jnp.int32, (128, 128), 0)
    dst = lax.broadcasted_iota(jnp.int32, (128, 128), 1)
    pairing = jnp.where(
        (src // width == dst // width) & ((src % width) // 2 == dst % BT), 0.125, 0.0
    ).astype(F32)
    partial = jnp.dot(
        fine_flux, pairing, precision=lax.Precision.HIGHEST, preferred_element_type=F32
    )
    for var in range(8):
        quad_v[quad_pos, pl.ds(var, 8, stride=8), :] = partial[var * 8 : var * 8 + 8]

    loads[1].wait()

    def to_primitive(step, edge):
        z = depth - 1 - step
        at = pl.multiple_of(z * width, width)
        edge = pltpu.roll(edge, width, 1)
        for half in range(2):
            prims = primitive([x_v[f, pl.ds(at + half * 8, 8), :] for f in range(8)])
            for f, value in enumerate(prims):
                prim_v[f, pl.ds(at + 2 * width + half * 8, 8), :] = value
                cross_v[f, pl.ds((2 + half * 8) * depth + z, 8, stride=depth), :] = value
                place = half * 8 + f
                moved = pltpu.roll(value, place, 1) if place else value
                edge = jnp.where(lane == place, -moved if f in FLIPPED else moved, edge)
        return edge

    edge_v[...] = lax.fori_loop(0, depth, to_primitive, jnp.zeros((8, 128), F32))

    for item in loads[2:]:
        item.wait()
    pl.semaphore_wait(barrier, greeted)

    def remote(src, dst, send, recv, t, g):
        return pltpu.make_async_remote_copy(
            src_ref=src, dst_ref=dst, send_sem=send, recv_sem=recv,
            device_id={"theta": t, "gz": g}, device_id_type=MESH,
        )

    across = remote(
        edge_v, edge_in, halo_send.at[0], halo_recv.at[0], (theta + theta_n // 2) % theta_n, gz
    )
    across.start()
    quad_copies = []
    for step in range(1, QUAD):
        copy = remote(
            quad_v.at[quad_pos], quad_v.at[quad_pos], quad_send.at[step], quad_recv.at[step],
            ring_pos * QUAD + (quad_pos + step) % QUAD, gz,
        )
        copy.start()
        quad_copies.append(copy)
    two_z, two_t = 2 * width, 2 * depth
    up = remote(
        prim_v.at[:, pl.ds(rows, two_z)], prim_v.at[:, pl.ds(0, two_z)],
        halo_send.at[1], halo_recv.at[1], theta, (gz + 1) % gz_n,
    )
    down = remote(
        prim_v.at[:, pl.ds(two_z, two_z)], prim_v.at[:, pl.ds(rows + two_z, two_z)],
        halo_send.at[2], halo_recv.at[2], theta, (gz + gz_n - 1) % gz_n,
    )
    not_last, not_first = gz < gz_n - 1, gz > 0
    pl.when(not_last)(up.start)
    pl.when(not_first)(down.start)
    ahead = remote(
        cross_v.at[:, pl.ds(rows, two_t)], cross_v.at[:, pl.ds(0, two_t)],
        halo_send.at[3], halo_recv.at[3], (theta + 1) % theta_n, gz,
    )
    back = remote(
        cross_v.at[:, pl.ds(two_t, two_t)], cross_v.at[:, pl.ds(rows + two_t, two_t)],
        halo_send.at[4], halo_recv.at[4], (theta + theta_n - 1) % theta_n, gz,
    )
    ahead.start()
    back.start()

    @pl.when(gz == 0)
    def _():
        for f in range(8):
            plane = prim_v[f, pl.ds(two_z, width), :]
            prim_v[f, pl.ds(0, width), :] = plane
            prim_v[f, pl.ds(width, width), :] = plane

    @pl.when(gz == gz_n - 1)
    def _():
        for f in range(8):
            plane = prim_v[f, pl.ds(rows + width, width), :]
            prim_v[f, pl.ds(rows + 2 * width, width), :] = plane
            prim_v[f, pl.ds(rows + 3 * width, width), :] = plane

    radius = lane.astype(F32) + 0.5
    inv_radius = 1.0 / radius
    inward = 0.5 * (radius - 0.5) * inv_radius
    outward = 0.5 * (radius + 0.5) * inv_radius
    turn = inv_radius * (0.5 / dtheta)
    pick = jnp.where(lane < 16, lane - 1, lane % BR)
    first, last = lane == 0, lane == 127

    across.wait()

    def radial(z, edge):
        at = pl.multiple_of(z * width, width)
        for half in range(2):
            left, right = [], []
            cell = [prim_v[f, pl.ds(at + two_z + half * 8, 8), :] for f in range(8)]
            for f in range(8):
                mid = cell[f]
                place = half * 8 + f
                inner = pltpu.roll(edge, 128 - place, 1) if place else edge
                lower = mid - jnp.where(first, inner, pltpu.roll(mid, 1, 1))
                upper = jnp.where(last, 0.0, pltpu.roll(lower, 127, 1))
                slope = half_slope(lower, upper)
                left.append(mid + slope)
                right.append(jnp.where(last, mid, pltpu.roll(mid - slope, 127, 1)))
            flux = double_flux(left, right, 0)
            rho, vr, vt, _, pressure, br, bt, bz = cell
            out = [inward * pltpu.roll(v, 1, 1) - outward * v for v in flux]
            field_sq = br * br + bt * bt + bz * bz
            out[1] = out[1] + inv_radius * (rho * vt * vt + pressure + 0.5 * field_sq - bt * bt)
            out[2] = out[2] - inv_radius * (rho * vr * vt - br * bt)
            out[6] = out[6] + inv_radius * (vr * bt - vt * br)
            packed = jnp.zeros((8, 128), F32)
            for f in range(8):
                res_ref[f, pl.ds(at + half * 8, 8), :] = out[f]
                packed = jnp.where(pick == f, pltpu.roll(flux[f], f + 1, 1), packed)
            packed_v[pl.ds(at + half * 8, 8), :] = packed
        return pltpu.roll(edge, 128 - width, 1)

    lax.fori_loop(0, depth, radial, edge_in[...])

    for copy in quad_copies:
        copy.wait()

    def spread(slot, totals):
        index = ring_pos * (QUAD * 8) + slot
        live = slot % 8 < count_s[ring_pos * QUAD + slot // 8]
        code = jnp.where(live, owner_s[index] * 2 + block_s[index], -1)
        relative = code - 2 * quad_pos - lane_block
        value = quad_v[slot // 8, pl.ds(pl.multiple_of(slot % 8 * 8, 8), 8), :]
        return tuple(
            total + jnp.where(relative == 2 * QUAD * k, value, 0.0)
            for k, total in enumerate(totals)
        )

    totals = lax.fori_loop(
        0, QUAD * 8, spread, tuple(jnp.zeros((8, 128), F32) for _ in range(ring_n))
    )
    for k in range(ring_n):
        out_v[k] = totals[k]
    ring_copies = []
    for step in ring_steps:
        to = (ring_pos + step) % ring_n
        copy = remote(
            out_v.at[to], in_v.at[ring_pos], ring_send.at[step], ring_recv.at[step],
            to * QUAD + quad_pos, gz,
        )
        copy.start()
        ring_copies.append(copy)

    def sweep(load_plane, faces, normal, emit):
        before, cell = load_plane(0), load_plane(1)
        after = load_plane(2)
        diff = [b - a for a, b in zip(before, cell)]
        diff_up = [b - a for a, b in zip(cell, after)]
        left = [c + half_slope(a, b) for a, b, c in zip(diff, diff_up, cell)]

        def face(k, carry):
            cell, diff, left, flux_low = carry
            after = load_plane(k + 3)
            diff_up = [b - a for a, b in zip(cell, after)]
            slope = [half_slope(a, b) for a, b in zip(diff, diff_up)]
            right = [c - s for c, s in zip(cell, slope)]
            flux = double_flux(left, right, normal)
            return after, diff_up, [c + s for c, s in zip(cell, slope)], flux

        carry = face(0, (after, diff_up, left, None))

        def body(k, carry):
            low = carry[3]
            carry = face(k, carry)
            emit(k - 1, [b - a for a, b in zip(low, carry[3])])
            return carry

        lax.fori_loop(1, faces, body, carry)

    ahead.wait()
    back.wait()

    def theta_plane(k):
        return [cross_v[f, pl.ds(pl.multiple_of(k * depth, depth), depth), :] for f in range(8)]

    def theta_emit(k, change):
        for f in range(8):
            at = pl.ds(k, depth, stride=width)
            res_ref[f, at, :] = res_ref[f, at, :] - turn * change[f]

    sweep(theta_plane, width + 1, 1, theta_emit)

    depth_of = [levels_s[b, 0] + levels_s[b, 1] + levels_s[b, 2] + levels_s[b, 3] for b in range(2)]
    turned_v[...] = packed_v[...].T
    for copy in ring_copies:
        copy.wait()
    registers = out_v[ring_pos]
    for step in range(1, ring_n):
        registers = registers + in_v[(ring_pos + step) % ring_n]
    level = jnp.where(lane_block == 0, depth_of[0], depth_of[1])
    coarse = jnp.where(
        level == 1,
        turned_v[BR : BR + 8, :],
        jnp.where(level == 2, turned_v[2 * BR : 2 * BR + 8, :], turned_v[3 * BR : 3 * BR + 8, :]),
    )
    mismatch = registers - 0.5 * coarse
    inner = 0.5 * turned_v[1:9, :]
    for z in range(depth):
        shift = (128 - z * width) % 128
        at = pl.ds(z, 8, stride=depth)
        mis_ref[at, :] = (pltpu.roll(mismatch, shift, 1) if shift else mismatch)[:, :width]
        inner_ref[at, :] = (pltpu.roll(inner, shift, 1) if shift else inner)[:, :width]
    face = (BR * level).astype(F32)
    corr_v[...] = jnp.concatenate([mismatch * (face / (face + 0.5))] * 16, axis=0).T

    @pl.when(not_first)
    def _():
        up.wait_recv()
        down.wait_send()

    @pl.when(not_last)
    def _():
        up.wait_send()
        down.wait_recv()

    for half in range(2):
        hit = lane == BR * depth_of[half]

        def axial_plane(k):
            at = pl.multiple_of(k * width + half * 8, 8)
            return [prim_v[f, pl.ds(at, 8), :] for f in range(8)]

        def axial_emit(k, change):
            at = pl.ds(pl.multiple_of(k * width + half * 8, 8), 8)
            corr = corr_v[at, :]
            for f in range(8):
                moved = pltpu.roll(corr, 128 - f, 1) if f else corr
                res_ref[f, at, :] = (
                    res_ref[f, at, :] - 0.5 * change[f] + jnp.where(hit, moved, 0.0)
                )

        sweep(axial_plane, depth + 1, 2, axial_emit)


def body(mesh_shape, fluid_state, levels, fine_rim, slot_owner, slot_block, slot_count):
    fields, depth, width, radial = fluid_state.shape
    theta_n, gz_n = mesh_shape
    rows = depth * width
    ring_n = theta_n // QUAD
    slots = fine_rim.shape[0]
    sizes = (theta_n, gz_n, depth, width, 2.0 * math.pi / (width * theta_n))
    hbm = pl.BlockSpec(memory_space=pltpu.MemorySpace.HBM)
    vmem = pl.BlockSpec(memory_space=pltpu.MemorySpace.VMEM)
    res, mis, inner = pl.pallas_call(
        functools.partial(kernel, sizes),
        out_shape=(
            jax.ShapeDtypeStruct((fields, rows, radial), F32),
            jax.ShapeDtypeStruct((fields * depth, width), F32),
            jax.ShapeDtypeStruct((fields * depth, width), F32),
        ),
        in_specs=[hbm] * 6,
        out_specs=(vmem, vmem, vmem),
        scratch_shapes=[
            pltpu.VMEM((fields, rows, radial), F32),
            pltpu.VMEM((slots * 2 * fields, 128), F32),
            pltpu.VMEM((fields, rows + 4 * width, radial), F32),
            pltpu.VMEM((fields, rows + 4 * depth, radial), F32),
            pltpu.VMEM((8, 128), F32),
            pltpu.VMEM((8, 128), F32),
            pltpu.VMEM((rows, 128), F32),
            pltpu.VMEM((128, rows), F32),
            pltpu.VMEM((rows, 128), F32),
            pltpu.VMEM((QUAD, slots * fields, 128), F32),
            pltpu.VMEM((ring_n, 8, 128), F32),
            pltpu.VMEM((ring_n, 8, 128), F32),
            pltpu.SMEM((2, 4), jnp.int32),
            pltpu.SMEM(slot_owner.shape, jnp.int32),
            pltpu.SMEM(slot_block.shape, jnp.int32),
            pltpu.SMEM(slot_count.shape, jnp.int32),
            pltpu.SemaphoreType.DMA((6,)),
            pltpu.SemaphoreType.DMA((QUAD,)),
            pltpu.SemaphoreType.DMA((QUAD,)),
            pltpu.SemaphoreType.DMA((ring_n,)),
            pltpu.SemaphoreType.DMA((ring_n,)),
            pltpu.SemaphoreType.DMA((5,)),
            pltpu.SemaphoreType.DMA((5,)),
        ],
        compiler_params=pltpu.CompilerParams(
            collective_id=0, has_side_effects=True, vmem_limit_bytes=32 * 1024 * 1024
        ),
    )(
        fluid_state.reshape(fields, rows, radial),
        fine_rim.reshape(slots * 2 * fields, 128),
        levels.T,
        slot_owner,
        slot_block,
        slot_count,
    )
    return (
        res.reshape(fields, depth, width, radial),
        mis.reshape(fields, depth, width),
        inner.reshape(fields, depth, width),
    )


def solution(mesh):
    return jax.shard_map(
        functools.partial(body, (mesh.shape["theta"], mesh.shape["gz"])),
        mesh=mesh,
        in_specs=(
            P(None, "gz", "theta", None),
            P(None, "theta"),
            P("theta", None, None, "gz"),
            P(),
            P(),
            P(),
        ),
        out_specs=(P(None, "gz", "theta", None), P(None, "gz", "theta"), P(None, "gz", "theta")),
        check_vma=False,
    )
```

time: 195 us -> 39.9 us (0.20)
  the two profiles are of different devices: /device:TPU:1 before, /device:TPU:20 now
where the time goes in v1:
time: 39.9 us; the launch traced here: 39.7 us
  Pallas kernels  34.4 us (86%)
  local copies, waits for them, and re-layouts  4.59 us (12%)
  between operations  0.68 us (2%)
    pallas_call x1, Pallas kernels, body(): pl.pallas_call(functools.partial(kernel, sizes), out_shape=(jax.ShapeDtyp...  34.4 us
    unnamed x15, local copies, waits for them, and re-layouts  4.59 us

profile of v1, /device:TPU:20, one launch (start us, length us, event | category | flops | bytes accessed | tf_op | source)
XLA Modules:
  0.0 39.7 jit_solution(3982563689640827086)
XLA Ops:
  0.6 0.0 copy-start.3
  0.6 0.0 copy-start.2
  0.7 0.0 copy-start.4
  0.7 0.0 copy-start.5
  0.7 0.6 %copy-done.3 = s32[512]{0:T(512)S(1)} copy-done((s32[512]{0:T(512)S(1)}, s32[512]{0:T(512)}, u32[]{:S(2)}) %copy-start.3) | copy-done | bytes 2072
  1.3 0.0 copy-done.2
  1.3 0.0 copy-done.4
  1.3 0.0 copy-done.5
  1.3 0.0 copy-start
  1.3 1.0 %copy-done = f32[8,8,16,128]{3,2,1,0:T(8,128)S(1)} copy-done((f32[8,8,16,128]{3,2,1,0:T(8,128)S(1)}, f32[8,8,16,128]{3,2,1,0:T(8,128)}, u32[]{:S(2)}) %copy-start) | copy-done | bytes 524312
  2.4 0.0 copy-start.1
  2.4 0.8 %copy-done.1 = f32[8,2,8,128]{3,2,1,0:T(8,128)S(1)} copy-done((f32[8,2,8,128]{3,2,1,0:T(8,128)S(1)}, f32[8,2,8,128]{3,2,1,0:T(8,128)}, u32[]{:S(2)}) %copy-start.1) | copy-done | bytes 65560
  3.2 34.4 %shard_map.85 = (f32[8,128,128]{2,1,0:T(8,128)S(1)}, f32[64,16]{1,0:T(8,128)S(1)}, f32[64,16]{1,0:T(8,128)S(1)}) custom-call(f32[8,128,128]{2,1,0:T(8,128)S(1)} %bitcast.6, f32[128,128]{1,0:T(8,128)S(1)} %bitcast.8, s32[2,4]{1,0:T(2,128)S(1)} %bitcast.11, s32[512]{0:T(512)S(1)} %copy-done.2, s32[512]{0:T(512)S(1)} %copy-done.3, s32[64]{0:T(128)S(1)} %copy-done.5), custom_call_target="tpu_custom_call" | custom-call | tf_op jit(solution)/shard_map/pallas_call | solution.py:388
  37.7 0.8 %copy.12 = f32[8,8,16,128]{3,2,1,0:T(8,128)} copy(f32[8,8,16,128]{3,2,1,0:T(8,128)S(1)} %bitcast.7) | data formatting | bytes 1048576
  38.5 0.6 %copy.13 = f32[8,8,16]{2,1,0:T(8,128)} copy(f32[8,8,16]{2,1,0:T(8,128)S(1)} %bitcast.10) | data formatting | bytes 8192
  39.1 0.6 %copy.14 = f32[8,8,16]{2,1,0:T(8,128)} copy(f32[8,8,16]{2,1,0:T(8,128)S(1)} %bitcast.9) | data formatting | bytes 8192
Async XLA Ops:
  0.6 0.7 %copy-start.3 = (s32[512]{0:T(512)S(1)}, s32[512]{0:T(512)}, u32[]{:S(2)}) copy-start(s32[512]{0:T(512)} %block_hbm.1) | copy-start | bytes 6148
  0.6 0.7 %copy-start.2 = (s32[512]{0:T(512)S(1)}, s32[512]{0:T(512)}, u32[]{:S(2)}) copy-start(s32[512]{0:T(512)} %owner_hbm.1) | copy-start | bytes 6148
  0.7 0.7 %copy-start.4 = (s32[4,2]{0,1:T(2,128)S(1)}, s32[4,2]{0,1:T(2,128)}, u32[]{:S(2)}) copy-start(s32[4,2]{0,1:T(2,128)} %param.7) | copy-start | bytes 100
  0.7 0.7 %copy-start.5 = (s32[64]{0:T(128)S(1)}, s32[64]{0:T(128)}, u32[]{:S(2)}) copy-start(s32[64]{0:T(128)} %count_hbm.1) | copy-start | bytes 772
  1.3 1.0 %copy-start = (f32[8,8,16,128]{3,2,1,0:T(8,128)S(1)}, f32[8,8,16,128]{3,2,1,0:T(8,128)}, u32[]{:S(2)}) copy-start(f32[8,8,16,128]{3,2,1,0:T(8,128)} %param.6) | copy-start | bytes 1572868
  2.4 0.8 %copy-start.1 = (f32[8,2,8,128]{3,2,1,0:T(8,128)S(1)}, f32[8,2,8,128]{3,2,1,0:T(8,128)}, u32[]{:S(2)}) copy-start(f32[8,2,8,128]{3,2,1,0:T(8,128)} %param.8) | copy-start | bytes 196612

commit v2 on v1

--- a/solution.py
+++ b/solution.py
@@ -11,7 +11,6 @@
 BT = 8
 BR = 32
 GAMMA = 5.0 / 3.0
-FLIPPED = (1, 2, 5, 6)
 QUAD = 4
 F32 = jnp.float32
 MESH = pl.DeviceIdType.MESH
@@ -141,24 +140,71 @@
 
     loads[1].wait()
 
-    def to_primitive(step, edge):
-        z = depth - 1 - step
+    def to_primitive(z, _):
         at = pl.multiple_of(z * width, width)
-        edge = pltpu.roll(edge, width, 1)
         for half in range(2):
             prims = primitive([x_v[f, pl.ds(at + half * 8, 8), :] for f in range(8)])
             for f, value in enumerate(prims):
                 prim_v[f, pl.ds(at + 2 * width + half * 8, 8), :] = value
                 cross_v[f, pl.ds((2 + half * 8) * depth + z, 8, stride=depth), :] = value
-                place = half * 8 + f
-                moved = pltpu.roll(value, place, 1) if place else value
-                edge = jnp.where(lane == place, -moved if f in FLIPPED else moved, edge)
-        return edge
-
-    edge_v[...] = lax.fori_loop(0, depth, to_primitive, jnp.zeros((8, 128), F32))
+        return 0
+
+    lax.fori_loop(0, depth, to_primitive, 0)
 
     for item in loads[2:]:
         item.wait()
+
+    radius = lane.astype(F32) + 0.5
+    inv_radius = 1.0 / radius
+    inward = jnp.where(lane == 1, 0.0, 0.5 * (radius - 0.5) * inv_radius)
+    outward = jnp.where(lane == 0, 0.0, 0.5 * (radius + 0.5) * inv_radius)
+    turn = inv_radius * (0.5 / dtheta)
+    last = lane == 127
+    spot = jnp.where(lane >= BR, lane % BR, -1)
+
+    def radial(z, _):
+        for half in range(2):
+            at = pl.multiple_of(z * width + half * 8, 8)
+            left, right = [], []
+            cell = [prim_v[f, pl.ds(at + 2 * width, 8), :] for f in range(8)]
+            packed = jnp.zeros((8, 128), F32)
+            for f in range(8):
+                mid = cell[f]
+                lower = mid - pltpu.roll(mid, 1, 1)
+                upper = jnp.where(last, 0.0, pltpu.roll(lower, 127, 1))
+                slope = half_slope(lower, upper)
+                left.append(mid + slope)
+                right.append(jnp.where(last, mid, pltpu.roll(mid - slope, 127, 1)))
+                packed = jnp.where(lane == f, pltpu.roll(mid, f, 1) if f else mid, packed)
+                packed = jnp.where(lane == f + 8, pltpu.roll(upper, f + 8, 1), packed)
+                packed = jnp.where(lane == f + 16, pltpu.roll(right[f], f + 16, 1), packed)
+            flux = double_flux(left, right, 0)
+            rho, vr, vt, _, pressure, br, bt, bz = cell
+            out = [inward * pltpu.roll(v, 1, 1) - outward * v for v in flux]
+            field_sq = br * br + bt * bt + bz * bz
+            out[1] = out[1] + inv_radius * (rho * vt * vt + pressure + 0.5 * field_sq - bt * bt)
+            out[2] = out[2] - inv_radius * (rho * vr * vt - br * bt)
+            out[6] = out[6] + inv_radius * (vr * bt - vt * br)
+            for f in range(8):
+                res_ref[f, pl.ds(at, 8), :] = out[f]
+                packed = jnp.where(spot == f, pltpu.roll(flux[f], f + 1, 1), packed)
+            packed_v[pl.ds(at, 8), :] = packed
+        return 0
+
+    lax.fori_loop(0, depth, radial, 0)
+    turned_v[...] = packed_v[...].T
+    row = lax.broadcasted_iota(jnp.int32, (8, 128), 0)
+    flip = (row == 1) | (row == 2) | (row == 5) | (row == 6)
+    edge_v[...] = jnp.where(flip, -turned_v[0:8, :], turned_v[0:8, :])
+
+    depth_of = [levels_s[b, 0] + levels_s[b, 1] + levels_s[b, 2] + levels_s[b, 3] for b in range(2)]
+    level = jnp.where(lane_block == 0, depth_of[0], depth_of[1])
+    coarse = 0.5 * jnp.where(
+        level == 1,
+        turned_v[BR : BR + 8, :],
+        jnp.where(level == 2, turned_v[2 * BR : 2 * BR + 8, :], turned_v[3 * BR : 3 * BR + 8, :]),
+    )
+
     pl.semaphore_wait(barrier, greeted)
 
     def remote(src, dst, send, recv, t, g):
@@ -167,10 +213,6 @@
             device_id={"theta": t, "gz": g}, device_id_type=MESH,
         )
 
-    across = remote(
-        edge_v, edge_in, halo_send.at[0], halo_recv.at[0], (theta + theta_n // 2) % theta_n, gz
-    )
-    across.start()
     quad_copies = []
     for step in range(1, QUAD):
         copy = remote(
@@ -179,6 +221,10 @@
         )
         copy.start()
         quad_copies.append(copy)
+    across = remote(
+        edge_v, edge_in, halo_send.at[0], halo_recv.at[0], (theta + theta_n // 2) % theta_n, gz
+    )
+    across.start()
     two_z, two_t = 2 * width, 2 * depth
     up = remote(
         prim_v.at[:, pl.ds(rows, two_z)], prim_v.at[:, pl.ds(0, two_z)],
@@ -215,46 +261,6 @@
             plane = prim_v[f, pl.ds(rows + width, width), :]
             prim_v[f, pl.ds(rows + 2 * width, width), :] = plane
             prim_v[f, pl.ds(rows + 3 * width, width), :] = plane
-
-    radius = lane.astype(F32) + 0.5
-    inv_radius = 1.0 / radius
-    inward = 0.5 * (radius - 0.5) * inv_radius
-    outward = 0.5 * (radius + 0.5) * inv_radius
-    turn = inv_radius * (0.5 / dtheta)
-    pick = jnp.where(lane < 16, lane - 1, lane % BR)
-    first, last = lane == 0, lane == 127
-
-    across.wait()
-
-    def radial(z, edge):
-        at = pl.multiple_of(z * width, width)
-        for half in range(2):
-            left, right = [], []
-            cell = [prim_v[f, pl.ds(at + two_z + half * 8, 8), :] for f in range(8)]
-            for f in range(8):
-                mid = cell[f]
-                place = half * 8 + f
-                inner = pltpu.roll(edge, 128 - place, 1) if place else edge
-                lower = mid - jnp.where(first, inner, pltpu.roll(mid, 1, 1))
-                upper = jnp.where(last, 0.0, pltpu.roll(lower, 127, 1))
-                slope = half_slope(lower, upper)
-                left.append(mid + slope)
-                right.append(jnp.where(last, mid, pltpu.roll(mid - slope, 127, 1)))
-            flux = double_flux(left, right, 0)
-            rho, vr, vt, _, pressure, br, bt, bz = cell
-            out = [inward * pltpu.roll(v, 1, 1) - outward * v for v in flux]
-            field_sq = br * br + bt * bt + bz * bz
-            out[1] = out[1] + inv_radius * (rho * vt * vt + pressure + 0.5 * field_sq - bt * bt)
-            out[2] = out[2] - inv_radius * (rho * vr * vt - br * bt)
-            out[6] = out[6] + inv_radius * (vr * bt - vt * br)
-            packed = jnp.zeros((8, 128), F32)
-            for f in range(8):
-                res_ref[f, pl.ds(at + half * 8, 8), :] = out[f]
-                packed = jnp.where(pick == f, pltpu.roll(flux[f], f + 1, 1), packed)
-            packed_v[pl.ds(at + half * 8, 8), :] = packed
-        return pltpu.roll(edge, 128 - width, 1)
-
-    lax.fori_loop(0, depth, radial, edge_in[...])
 
     for copy in quad_copies:
         copy.wait()
@@ -324,56 +330,82 @@
 
     sweep(theta_plane, width + 1, 1, theta_emit)
 
-    depth_of = [levels_s[b, 0] + levels_s[b, 1] + levels_s[b, 2] + levels_s[b, 3] for b in range(2)]
-    turned_v[...] = packed_v[...].T
+    @pl.when(not_first)
+    def _():
+        up.wait_recv()
+        down.wait_send()
+
+    @pl.when(not_last)
+    def _():
+        up.wait_send()
+        down.wait_recv()
+
+    for half in range(2):
+
+        def axial_plane(k):
+            at = pl.multiple_of(k * width + half * 8, 8)
+            return [prim_v[f, pl.ds(at, 8), :] for f in range(8)]
+
+        def axial_emit(k, change):
+            at = pl.ds(pl.multiple_of(k * width + half * 8, 8), 8)
+            for f in range(8):
+                res_ref[f, at, :] = res_ref[f, at, :] - 0.5 * change[f]
+
+        sweep(axial_plane, depth + 1, 2, axial_emit)
+
+    across.wait()
+    cell = [turned_v[f : f + 1, :] for f in range(8)]
+    left = [
+        cell[f]
+        + half_slope(cell[f] - edge_in[f : f + 1, :], turned_v[8 + f : 9 + f, :])
+        for f in range(8)
+    ]
+    face_one = double_flux(left, [turned_v[16 + f : 17 + f, :] for f in range(8)], 0)
+
     for copy in ring_copies:
         copy.wait()
     registers = out_v[ring_pos]
     for step in range(1, ring_n):
         registers = registers + in_v[(ring_pos + step) % ring_n]
-    level = jnp.where(lane_block == 0, depth_of[0], depth_of[1])
-    coarse = jnp.where(
-        level == 1,
-        turned_v[BR : BR + 8, :],
-        jnp.where(level == 2, turned_v[2 * BR : 2 * BR + 8, :], turned_v[3 * BR : 3 * BR + 8, :]),
-    )
-    mismatch = registers - 0.5 * coarse
-    inner = 0.5 * turned_v[1:9, :]
+    mismatch = registers - coarse
+    inner = jnp.concatenate([0.5 * v for v in face_one], axis=0)
     for z in range(depth):
         shift = (128 - z * width) % 128
         at = pl.ds(z, 8, stride=depth)
         mis_ref[at, :] = (pltpu.roll(mismatch, shift, 1) if shift else mismatch)[:, :width]
         inner_ref[at, :] = (pltpu.roll(inner, shift, 1) if shift else inner)[:, :width]
     face = (BR * level).astype(F32)
-    corr_v[...] = jnp.concatenate([mismatch * (face / (face + 0.5))] * 16, axis=0).T
-
-    @pl.when(not_first)
-    def _():
-        up.wait_recv()
-        down.wait_send()
-
-    @pl.when(not_last)
-    def _():
-        up.wait_send()
-        down.wait_recv()
-
-    for half in range(2):
-        hit = lane == BR * depth_of[half]
-
-        def axial_plane(k):
-            at = pl.multiple_of(k * width + half * 8, 8)
-            return [prim_v[f, pl.ds(at, 8), :] for f in range(8)]
-
-        def axial_emit(k, change):
-            at = pl.ds(pl.multiple_of(k * width + half * 8, 8), 8)
+    added = mismatch * (face / (face + 0.5))
+    nothing = jnp.zeros((1, 128), F32)
+    inner_part, outer_part = [], []
+    for f in range(8):
+        inner_part += [-face_one[f], face_one[f] * (1.0 / 3.0), nothing, nothing]
+        outer_part += [added[f : f + 1], nothing, nothing, nothing]
+    corr_v[...] = jnp.concatenate(inner_part + outer_part * 3, axis=0).T
+
+    hits = [(lane < 2) | (lane == BR * depth_of[half]) for half in range(2)]
+
+    def correct(z, _):
+        for half in range(2):
+            at = pl.ds(pl.multiple_of(z * width + half * 8, 8), 8)
             corr = corr_v[at, :]
             for f in range(8):
-                moved = pltpu.roll(corr, 128 - f, 1) if f else corr
-                res_ref[f, at, :] = (
-                    res_ref[f, at, :] - 0.5 * change[f] + jnp.where(hit, moved, 0.0)
-                )
-
-        sweep(axial_plane, depth + 1, 2, axial_emit)
+                moved = pltpu.roll(corr, 128 - 4 * f, 1) if f else corr
+                res_ref[f, at, :] = res_ref[f, at, :] + jnp.where(hits[half], moved, 0.0)
+        return 0
+
+    lax.fori_loop(0, depth, correct, 0)
+
+
+def copy_out(*refs):
+    count = len(refs) // 2
+    copies = [
+        pltpu.make_async_copy(refs[i], refs[count + i], refs[-1].at[i]) for i in range(count)
+    ]
+    for copy in copies:
+        copy.start()
+    for copy in copies:
+        copy.wait()
 
 
 def body(mesh_shape, fluid_state, levels, fine_rim, slot_owner, slot_block, slot_count):
@@ -423,13 +455,27 @@
             collective_id=0, has_side_effects=True, vmem_limit_bytes=32 * 1024 * 1024
         ),
     )(
-        fluid_state.reshape(fields, rows, radial),
-        fine_rim.reshape(slots * 2 * fields, 128),
-        levels.T,
-        slot_owner,
-        slot_block,
-        slot_count,
-    )
+        *(
+            pltpu.with_memory_space_constraint(v, pltpu.MemorySpace.HBM)
+            for v in (
+                fluid_state.reshape(fields, rows, radial),
+                fine_rim.reshape(slots * 2 * fields, 128),
+                levels.T,
+                slot_owner,
+                slot_block,
+                slot_count,
+            )
+        )
+    )
+    outs = (res, mis, inner)
+    res, mis, inner = pl.pallas_call(
+        copy_out,
+        out_shape=tuple(jax.ShapeDtypeStruct(v.shape, F32) for v in outs),
+        in_specs=[vmem] * 3,
+        out_specs=(hbm,) * 3,
+        scratch_shapes=[pltpu.SemaphoreType.DMA((3,))],
+        compiler_params=pltpu.CompilerParams(vmem_limit_bytes=2 * 1024 * 1024),
+    )(*outs)
     return (
         res.reshape(fields, depth, width, radial),
         mis.reshape(fields, depth, width),

time: 39.9 us -> 33.6 us (0.84)
  the two profiles are of different devices: /device:TPU:20 before, /device:TPU:1 now
where the time goes in v2:
time: 33.6 us; the launch traced here: 33.5 us
  Pallas kernels  32.9 us (98%)
  between operations  0.64 us (2%)
    pallas_call x1, Pallas kernels, body(): pl.pallas_call(functools.partial(kernel, sizes), out_shape=(jax.ShapeDtyp...  32 us
    pallas_call x1, Pallas kernels, body(): pl.pallas_call(copy_out, out_shape=tuple((jax.ShapeDtypeStruct(v.shape, F...  0.83 us

profile of v2, /device:TPU:1, one launch (start us, length us, event | category | flops | bytes accessed | tf_op | source)
XLA Modules:
  0.0 33.5 jit_solution(6131176393375322245)
XLA Ops:
  0.6 32.0 %shard_map.85 = (f32[8,128,128]{2,1,0:T(8,128)S(1)}, f32[64,16]{1,0:T(8,128)S(1)}, f32[64,16]{1,0:T(8,128)S(1)}) custom-call(f32[8,128,128]{2,1,0:T(8,128)} %bitcast.6, f32[128,128]{1,0:T(8,128)} %bitcast.7, s32[2,4]{1,0:T(2,128)} %bitcast.8, s32[512]{0:T(512)} %owner_hbm.1, s32[512]{0:T(512)} %block_hbm.1, s32[64]{0:T(128)} %count_hbm.1), custom_call_target="tpu_custom_call" | custom-call | tf_op jit(solution)/shard_map/pallas_call | solution.py:420
  32.7 0.8 %shard_map.86 = (f32[8,128,128]{2,1,0:T(8,128)}, f32[64,16]{1,0:T(8,128)}, f32[64,16]{1,0:T(8,128)}) custom-call(f32[8,128,128]{2,1,0:T(8,128)S(1)} %get-tuple-element.9.refs_0_, f32[64,16]{1,0:T(8,128)S(1)} %get-tuple-element.10.refs_1_, f32[64,16]{1,0:T(8,128)S(1)} %get-tuple-element.11.refs_2_), custom_call_target="tpu_custom_call" | custom-call | tf_op jit(solution)/shard_map/pallas_call | solution.py:471

commit v3 on v2

--- a/solution.py
+++ b/solution.py
@@ -74,7 +74,7 @@
     x_v, fine_v, prim_v, cross_v, edge_v, edge_in, packed_v, turned_v, corr_v,
     quad_v, out_v, in_v,
     levels_s, owner_s, block_s, count_s,
-    load_sem, quad_send, quad_recv, ring_send, ring_recv, halo_send, halo_recv,
+    load_sem, quad_send, quad_recv, ring_send, ring_recv, halo_send, halo_recv, news_sem,
 ):
     theta_n, gz_n, depth, width, dtheta = sizes
     rows = depth * width
@@ -98,26 +98,34 @@
         item.start()
 
     barrier = pltpu.get_barrier_semaphore()
-    greeted = 0
-
-    def greet(t, g):
-        pl.semaphore_signal(barrier, inc=1, device_id={"theta": t, "gz": g}, device_id_type=MESH)
-
-    ring_steps = sorted(range(1, ring_n), key=lambda d: -min(d, ring_n - d))
-    for step in ring_steps:
-        greet((ring_pos + step) % ring_n * QUAD + quad_pos, gz)
-        greeted += 1
-    for t, g in (
-        ((theta + 1) % theta_n, gz),
-        ((theta + theta_n - 1) % theta_n, gz),
-        (theta, (gz + 1) % gz_n),
-        (theta, (gz + gz_n - 1) % gz_n),
-    ):
-        greet(t, g)
-        greeted += 1
-    for step in range(1, QUAD):
-        greet(ring_pos * QUAD + (quad_pos + step) % QUAD, gz)
-        greeted += 1
+    half_n = ring_n // 2
+    early = ring_pos < half_n
+    half_at = ring_pos // half_n * half_n
+
+    def signal(sem, t, g):
+        pl.semaphore_signal(sem, inc=1, device_id={"theta": t, "gz": g}, device_id_type=MESH)
+
+    def same_ring(step):
+        return half_at + (ring_pos - half_at + step) % half_n
+
+    def other_ring(step):
+        return half_n - half_at + (ring_pos - half_at + step) % half_n
+
+    def hear(role, count):
+        @pl.when(quad_pos == role)
+        def _():
+            pl.semaphore_wait(barrier, count)
+            for step in range(1, QUAD):
+                signal(news_sem.at[role], ring_pos * QUAD + (role + step) % QUAD, gz)
+
+    def heed(role):
+        @pl.when(quad_pos != role)
+        def _():
+            pl.semaphore_wait(news_sem.at[role], 1)
+
+    @pl.when(quad_pos != 0)
+    def _():
+        signal(barrier, ring_pos * QUAD, gz)
 
     lane = lax.broadcasted_iota(jnp.int32, (8, 128), 1)
     lane_block = (lane % width) // BT
@@ -138,6 +146,8 @@
     for var in range(8):
         quad_v[quad_pos, pl.ds(var, 8, stride=8), :] = partial[var * 8 : var * 8 + 8]
 
+    hear(0, QUAD - 1)
+
     loads[1].wait()
 
     def to_primitive(z, _):
@@ -153,6 +163,42 @@
 
     for item in loads[2:]:
         item.wait()
+    heed(0)
+
+    @pl.when(quad_pos == 1)
+    def _():
+        for step in range(1, half_n):
+            signal(barrier, same_ring(step) * QUAD + 1, gz)
+
+    @pl.when(quad_pos == 2)
+    def _():
+        for step in range(half_n):
+            signal(barrier, other_ring(step) * QUAD + 2, gz)
+
+    @pl.when(quad_pos == 3)
+    def _():
+        for t, g in (
+            ((theta + QUAD) % theta_n, gz),
+            ((theta + theta_n - QUAD) % theta_n, gz),
+            (theta, (gz + 1) % gz_n),
+            (theta, (gz + gz_n - 1) % gz_n),
+        ):
+            signal(barrier, t, g)
+
+    def remote(src, dst, send, recv, t, g):
+        return pltpu.make_async_remote_copy(
+            src_ref=src, dst_ref=dst, send_sem=send, recv_sem=recv,
+            device_id={"theta": t, "gz": g}, device_id_type=MESH,
+        )
+
+    quad_copies = []
+    for step in range(1, QUAD):
+        copy = remote(
+            quad_v.at[quad_pos], quad_v.at[quad_pos], quad_send.at[step], quad_recv.at[step],
+            ring_pos * QUAD + (quad_pos + step) % QUAD, gz,
+        )
+        copy.start()
+        quad_copies.append(copy)
 
     radius = lane.astype(F32) + 0.5
     inv_radius = 1.0 / radius
@@ -205,26 +251,9 @@
         jnp.where(level == 2, turned_v[2 * BR : 2 * BR + 8, :], turned_v[3 * BR : 3 * BR + 8, :]),
     )
 
-    pl.semaphore_wait(barrier, greeted)
-
-    def remote(src, dst, send, recv, t, g):
-        return pltpu.make_async_remote_copy(
-            src_ref=src, dst_ref=dst, send_sem=send, recv_sem=recv,
-            device_id={"theta": t, "gz": g}, device_id_type=MESH,
-        )
-
-    quad_copies = []
-    for step in range(1, QUAD):
-        copy = remote(
-            quad_v.at[quad_pos], quad_v.at[quad_pos], quad_send.at[step], quad_recv.at[step],
-            ring_pos * QUAD + (quad_pos + step) % QUAD, gz,
-        )
-        copy.start()
-        quad_copies.append(copy)
     across = remote(
         edge_v, edge_in, halo_send.at[0], halo_recv.at[0], (theta + theta_n // 2) % theta_n, gz
     )
-    across.start()
     two_z, two_t = 2 * width, 2 * depth
     up = remote(
         prim_v.at[:, pl.ds(rows, two_z)], prim_v.at[:, pl.ds(0, two_z)],
@@ -235,8 +264,6 @@
         halo_send.at[2], halo_recv.at[2], theta, (gz + gz_n - 1) % gz_n,
     )
     not_last, not_first = gz < gz_n - 1, gz > 0
-    pl.when(not_last)(up.start)
-    pl.when(not_first)(down.start)
     ahead = remote(
         cross_v.at[:, pl.ds(rows, two_t)], cross_v.at[:, pl.ds(0, two_t)],
         halo_send.at[3], halo_recv.at[3], (theta + 1) % theta_n, gz,
@@ -245,8 +272,12 @@
         cross_v.at[:, pl.ds(two_t, two_t)], cross_v.at[:, pl.ds(rows + two_t, two_t)],
         halo_send.at[4], halo_recv.at[4], (theta + theta_n - 1) % theta_n, gz,
     )
-    ahead.start()
-    back.start()
+
+    def send_halos():
+        ahead.start()
+        back.start()
+        pl.when(not_last)(up.start)
+        pl.when(not_first)(down.start)
 
     @pl.when(gz == 0)
     def _():
@@ -261,6 +292,9 @@
             plane = prim_v[f, pl.ds(rows + width, width), :]
             prim_v[f, pl.ds(rows + 2 * width, width), :] = plane
             prim_v[f, pl.ds(rows + 3 * width, width), :] = plane
+
+    hear(3, 4)
+    heed(3)
 
     for copy in quad_copies:
         copy.wait()
@@ -281,15 +315,39 @@
     )
     for k in range(ring_n):
         out_v[k] = totals[k]
-    ring_copies = []
-    for step in ring_steps:
-        to = (ring_pos + step) % ring_n
-        copy = remote(
-            out_v.at[to], in_v.at[ring_pos], ring_send.at[step], ring_recv.at[step],
+
+    def ring_copy(to, slot):
+        return remote(
+            out_v.at[to], in_v.at[ring_pos], ring_send.at[slot], ring_recv.at[slot],
             to * QUAD + quad_pos, gz,
         )
+
+    same_copies = [ring_copy(same_ring(step), step) for step in range(1, half_n)]
+    other_copies = [ring_copy(other_ring(step), half_n + step) for step in range(half_n)]
+
+    def send_same():
+        hear(1, half_n - 1)
+        heed(1)
+        for copy in same_copies:
+            copy.start()
+
+    @pl.when(early)
+    def _():
+        send_halos()
+        send_same()
+
+    hear(2, half_n)
+    heed(2)
+    for copy in other_copies:
         copy.start()
-        ring_copies.append(copy)
+    across.start()
+
+    @pl.when(jnp.logical_not(early))
+    def _():
+        send_halos()
+        send_same()
+
+    ring_copies = same_copies + other_copies
 
     def sweep(load_plane, faces, normal, emit):
         before, cell = load_plane(0), load_plane(1)
@@ -450,6 +508,7 @@
             pltpu.SemaphoreType.DMA((ring_n,)),
             pltpu.SemaphoreType.DMA((5,)),
             pltpu.SemaphoreType.DMA((5,)),
+            pltpu.SemaphoreType.REGULAR((4,)),
         ],
         compiler_params=pltpu.CompilerParams(
             collective_id=0, has_side_effects=True, vmem_limit_bytes=32 * 1024 * 1024

time: 33.6 us -> 30.9 us (0.920)
  the two profiles are of different devices: /device:TPU:1 before, /device:TPU:32 now
where the time goes in v3:
time: 30.9 us; the launch traced here: 30.8 us
  Pallas kernels  30.1 us (97%)
  between operations  0.64 us (2%)
    pallas_call x1, Pallas kernels, body(): pl.pallas_call(functools.partial(kernel, sizes), out_shape=(jax.ShapeDtyp...  29.3 us
    pallas_call x1, Pallas kernels, body(): pl.pallas_call(copy_out, out_shape=tuple((jax.ShapeDtypeStruct(v.shape, F...  0.83 us

profile of v3, /device:TPU:32, one launch (start us, length us, event | category | flops | bytes accessed | tf_op | source)
XLA Modules:
  0.0 30.8 jit_solution(13831149002141111847)
XLA Ops:
  0.6 29.3 %shard_map.85 = (f32[8,128,128]{2,1,0:T(8,128)S(1)}, f32[64,16]{1,0:T(8,128)S(1)}, f32[64,16]{1,0:T(8,128)S(1)}) custom-call(f32[8,128,128]{2,1,0:T(8,128)} %bitcast.6, f32[128,128]{1,0:T(8,128)} %bitcast.7, s32[2,4]{1,0:T(2,128)} %bitcast.8, s32[512]{0:T(512)} %owner_hbm.1, s32[512]{0:T(512)} %block_hbm.1, s32[64]{0:T(128)} %count_hbm.1), custom_call_target="tpu_custom_call" | custom-call | tf_op jit(solution)/shard_map/pallas_call | solution.py:478
  30.0 0.8 %shard_map.86 = (f32[8,128,128]{2,1,0:T(8,128)}, f32[64,16]{1,0:T(8,128)}, f32[64,16]{1,0:T(8,128)}) custom-call(f32[8,128,128]{2,1,0:T(8,128)S(1)} %get-tuple-element.9.refs_0_, f32[64,16]{1,0:T(8,128)S(1)} %get-tuple-element.10.refs_1_, f32[64,16]{1,0:T(8,128)S(1)} %get-tuple-element.11.refs_2_), custom_call_target="tpu_custom_call" | custom-call | tf_op jit(solution)/shard_map/pallas_call | solution.py:530

commit v4 on v3

--- a/solution.py
+++ b/solution.py
@@ -100,7 +100,11 @@
     barrier = pltpu.get_barrier_semaphore()
     half_n = ring_n // 2
     early = ring_pos < half_n
+    late = jnp.logical_not(early)
     half_at = ring_pos // half_n * half_n
+    core_zero = quad_pos % 2 == 0
+    not_start, not_end = ring_pos > half_at, ring_pos < half_at + half_n - 1
+    ring_near = not_start.astype(jnp.int32) + not_end.astype(jnp.int32)
 
     def signal(sem, t, g):
         pl.semaphore_signal(sem, inc=1, device_id={"theta": t, "gz": g}, device_id_type=MESH)
@@ -126,6 +130,10 @@
     @pl.when(quad_pos != 0)
     def _():
         signal(barrier, ring_pos * QUAD, gz)
+
+    @pl.when(late & (quad_pos != 2))
+    def _():
+        signal(barrier, ring_pos * QUAD + 2, gz)
 
     lane = lax.broadcasted_iota(jnp.int32, (8, 128), 1)
     lane_block = (lane % width) // BT
@@ -146,7 +154,12 @@
     for var in range(8):
         quad_v[quad_pos, pl.ds(var, 8, stride=8), :] = partial[var * 8 : var * 8 + 8]
 
-    hear(0, QUAD - 1)
+    pl.when(early)(functools.partial(hear, 0, QUAD - 1))
+
+    @pl.when(late & core_zero)
+    def _():
+        pl.semaphore_wait(barrier, QUAD - 1)
+        signal(news_sem.at[0], theta + 1, gz)
 
     loads[1].wait()
 
@@ -163,27 +176,10 @@
 
     for item in loads[2:]:
         item.wait()
-    heed(0)
-
-    @pl.when(quad_pos == 1)
-    def _():
-        for step in range(1, half_n):
-            signal(barrier, same_ring(step) * QUAD + 1, gz)
-
-    @pl.when(quad_pos == 2)
-    def _():
-        for step in range(half_n):
-            signal(barrier, other_ring(step) * QUAD + 2, gz)
-
-    @pl.when(quad_pos == 3)
-    def _():
-        for t, g in (
-            ((theta + QUAD) % theta_n, gz),
-            ((theta + theta_n - QUAD) % theta_n, gz),
-            (theta, (gz + 1) % gz_n),
-            (theta, (gz + gz_n - 1) % gz_n),
-        ):
-            signal(barrier, t, g)
+
+    @pl.when((early & (quad_pos != 0)) | (late & jnp.logical_not(core_zero)))
+    def _():
+        pl.semaphore_wait(news_sem.at[0], 1)
 
     def remote(src, dst, send, recv, t, g):
         return pltpu.make_async_remote_copy(
@@ -199,6 +195,27 @@
         )
         copy.start()
         quad_copies.append(copy)
+
+    gz_next, gz_back = (gz + 1) % gz_n, (gz + gz_n - 1) % gz_n
+
+    def greet_near():
+        signal(barrier, theta, gz_next)
+        signal(barrier, theta, gz_back)
+        pl.when(not_start)(functools.partial(signal, barrier, theta - QUAD, gz))
+        pl.when(not_end)(functools.partial(signal, barrier, theta + QUAD, gz))
+
+    @pl.when(quad_pos == 1)
+    def _():
+        for step in range(half_n):
+            signal(barrier, other_ring(step) * QUAD + 1, gz)
+        pl.when(late)(greet_near)
+
+    pl.when(early & (quad_pos == 2))(greet_near)
+
+    @pl.when(quad_pos == 3)
+    def _():
+        for step in range(1, half_n):
+            signal(barrier, same_ring(step) * QUAD + 3, gz)
 
     radius = lane.astype(F32) + 0.5
     inv_radius = 1.0 / radius
@@ -273,9 +290,12 @@
         halo_send.at[4], halo_recv.at[4], (theta + theta_n - 1) % theta_n, gz,
     )
 
+    ahead_waits = theta == theta_n // 2 - 1
+    back_waits = theta == 0
+
     def send_halos():
-        ahead.start()
-        back.start()
+        pl.when(jnp.logical_not(ahead_waits))(ahead.start)
+        pl.when(jnp.logical_not(back_waits))(back.start)
         pl.when(not_last)(up.start)
         pl.when(not_first)(down.start)
 
@@ -293,8 +313,13 @@
             prim_v[f, pl.ds(rows + 2 * width, width), :] = plane
             prim_v[f, pl.ds(rows + 3 * width, width), :] = plane
 
-    hear(3, 4)
-    heed(3)
+    @pl.when(early)
+    def _():
+        hear(2, 2 + ring_near)
+        heed(2)
+        send_halos()
+
+    pl.when(late)(functools.partial(hear, 1, half_n + 2 + ring_near))
 
     for copy in quad_copies:
         copy.wait()
@@ -326,28 +351,27 @@
     other_copies = [ring_copy(other_ring(step), half_n + step) for step in range(half_n)]
 
     def send_same():
-        hear(1, half_n - 1)
-        heed(1)
+        heed(3)
         for copy in same_copies:
             copy.start()
 
+    def send_other():
+        heed(1)
+        for copy in other_copies:
+            copy.start()
+        across.start()
+
     @pl.when(early)
     def _():
+        hear(3, half_n - 1)
+        send_same()
+
+    @pl.when(late)
+    def _():
+        send_other()
         send_halos()
+        hear(3, half_n - 1)
         send_same()
-
-    hear(2, half_n)
-    heed(2)
-    for copy in other_copies:
-        copy.start()
-    across.start()
-
-    @pl.when(jnp.logical_not(early))
-    def _():
-        send_halos()
-        send_same()
-
-    ring_copies = same_copies + other_copies
 
     def sweep(load_plane, faces, normal, emit):
         before, cell = load_plane(0), load_plane(1)
@@ -375,8 +399,38 @@
 
         lax.fori_loop(1, faces, body, carry)
 
-    ahead.wait()
-    back.wait()
+    @pl.when(not_first)
+    def _():
+        up.wait_recv()
+        down.wait_send()
+
+    @pl.when(not_last)
+    def _():
+        up.wait_send()
+        down.wait_recv()
+
+    for half in range(2):
+
+        def axial_plane(k):
+            at = pl.multiple_of(k * width + half * 8, 8)
+            return [prim_v[f, pl.ds(at, 8), :] for f in range(8)]
+
+        def axial_emit(k, change):
+            at = pl.ds(pl.multiple_of(k * width + half * 8, 8), 8)
+            for f in range(8):
+                res_ref[f, at, :] = res_ref[f, at, :] - 0.5 * change[f]
+
+        sweep(axial_plane, depth + 1, 2, axial_emit)
+
+    @pl.when(early)
+    def _():
+        hear(1, half_n)
+        send_other()
+        pl.when(ahead_waits)(ahead.start)
+        pl.when(back_waits)(back.start)
+
+    ahead.wait_recv()
+    back.wait_recv()
 
     def theta_plane(k):
         return [cross_v[f, pl.ds(pl.multiple_of(k * depth, depth), depth), :] for f in range(8)]
@@ -388,28 +442,8 @@
 
     sweep(theta_plane, width + 1, 1, theta_emit)
 
-    @pl.when(not_first)
-    def _():
-        up.wait_recv()
-        down.wait_send()
-
-    @pl.when(not_last)
-    def _():
-        up.wait_send()
-        down.wait_recv()
-
-    for half in range(2):
-
-        def axial_plane(k):
-            at = pl.multiple_of(k * width + half * 8, 8)
-            return [prim_v[f, pl.ds(at, 8), :] for f in range(8)]
-
-        def axial_emit(k, change):
-            at = pl.ds(pl.multiple_of(k * width + half * 8, 8), 8)
-            for f in range(8):
-                res_ref[f, at, :] = res_ref[f, at, :] - 0.5 * change[f]
-
-        sweep(axial_plane, depth + 1, 2, axial_emit)
+    ahead.wait_send()
+    back.wait_send()
 
     across.wait()
     cell = [turned_v[f : f + 1, :] for f in range(8)]
@@ -420,7 +454,7 @@
     ]
     face_one = double_flux(left, [turned_v[16 + f : 17 + f, :] for f in range(8)], 0)
 
-    for copy in ring_copies:
+    for copy in same_copies + other_copies:
         copy.wait()
     registers = out_v[ring_pos]
     for step in range(1, ring_n):
@@ -452,7 +486,7 @@
                 res_ref[f, at, :] = res_ref[f, at, :] + jnp.where(hits[half], moved, 0.0)
         return 0
 
-    lax.fori_loop(0, depth, correct, 0)
+    lax.fori_loop(0, depth, correct, 0, unroll=2)
 
 
 def copy_out(*refs):

time: 30.9 us -> 29.8 us (0.964)
  the two profiles are of different devices: /device:TPU:32 before, /device:TPU:472 now
where the time goes in v4:
time: 29.8 us; the launch traced here: 29.7 us
  Pallas kernels  29.1 us (98%)
  between operations  0.64 us (2%)
    pallas_call x1, Pallas kernels, body(): pl.pallas_call(functools.partial(kernel, sizes), out_shape=(jax.ShapeDtyp...  28.2 us
    pallas_call x1, Pallas kernels, body(): pl.pallas_call(copy_out, out_shape=tuple((jax.ShapeDtypeStruct(v.shape, F...  0.83 us

profile of v4, /device:TPU:472, one launch (start us, length us, event | category | flops | bytes accessed | tf_op | source)
XLA Modules:
  0.0 29.7 jit_solution(13767490436954252033)
XLA Ops:
  0.6 28.2 %shard_map.85 = (f32[8,128,128]{2,1,0:T(8,128)S(1)}, f32[64,16]{1,0:T(8,128)S(1)}, f32[64,16]{1,0:T(8,128)S(1)}) custom-call(f32[8,128,128]{2,1,0:T(8,128)} %bitcast.6, f32[128,128]{1,0:T(8,128)} %bitcast.7, s32[2,4]{1,0:T(2,128)} %bitcast.8, s32[512]{0:T(512)} %owner_hbm.1, s32[512]{0:T(512)} %block_hbm.1, s32[64]{0:T(128)} %count_hbm.1), custom_call_target="tpu_custom_call" | custom-call | tf_op jit(solution)/shard_map/pallas_call | solution.py:512
  28.9 0.8 %shard_map.86 = (f32[8,128,128]{2,1,0:T(8,128)}, f32[64,16]{1,0:T(8,128)}, f32[64,16]{1,0:T(8,128)}) custom-call(f32[8,128,128]{2,1,0:T(8,128)S(1)} %get-tuple-element.9.refs_0_, f32[64,16]{1,0:T(8,128)S(1)} %get-tuple-element.10.refs_1_, f32[64,16]{1,0:T(8,128)S(1)} %get-tuple-element.11.refs_2_), custom_call_target="tpu_custom_call" | custom-call | tf_op jit(solution)/shard_map/pallas_call | solution.py:564

commit v5 on v4

--- a/solution.py
+++ b/solution.py
@@ -101,6 +101,8 @@
     half_n = ring_n // 2
     early = ring_pos < half_n
     late = jnp.logical_not(early)
+    soon = ring_pos < half_n // 2
+    later = jnp.logical_not(soon)
     half_at = ring_pos // half_n * half_n
     core_zero = quad_pos % 2 == 0
     not_start, not_end = ring_pos > half_at, ring_pos < half_at + half_n - 1
@@ -131,7 +133,7 @@
     def _():
         signal(barrier, ring_pos * QUAD, gz)
 
-    @pl.when(late & (quad_pos != 2))
+    @pl.when(later & (quad_pos != 2))
     def _():
         signal(barrier, ring_pos * QUAD + 2, gz)
 
@@ -152,14 +154,63 @@
         fine_flux, pairing, precision=lax.Precision.HIGHEST, preferred_element_type=F32
     )
     for var in range(8):
-        quad_v[quad_pos, pl.ds(var, 8, stride=8), :] = partial[var * 8 : var * 8 + 8]
-
-    pl.when(early)(functools.partial(hear, 0, QUAD - 1))
-
-    @pl.when(late & core_zero)
-    def _():
-        pl.semaphore_wait(barrier, QUAD - 1)
-        signal(news_sem.at[0], theta + 1, gz)
+        rows_var = partial[var * 8 : var * 8 + 8]
+        pair = jnp.where(lane_block == 0, rows_var, pltpu.roll(rows_var, 4, 0))
+        quad_v[quad_pos, pl.ds(var, 4, stride=8), :] = pair[0:4]
+
+    def remote(src, dst, send, recv, t, g):
+        return pltpu.make_async_remote_copy(
+            src_ref=src, dst_ref=dst, send_sem=send, recv_sem=recv,
+            device_id={"theta": t, "gz": g}, device_id_type=MESH,
+        )
+
+    partners = [quad_pos + 1 - 2 * (quad_pos % 2), (quad_pos + 2) % QUAD, QUAD - 1 - quad_pos]
+    quad_copies = [
+        remote(
+            quad_v.at[quad_pos], quad_v.at[quad_pos], quad_send.at[i], quad_recv.at[i],
+            ring_pos * QUAD + partner, gz,
+        )
+        for i, partner in enumerate(partners)
+    ]
+    gz_next, gz_back = (gz + 1) % gz_n, (gz + gz_n - 1) % gz_n
+
+    def greet_near():
+        signal(barrier, theta, gz_next)
+        signal(barrier, theta, gz_back)
+        for there, r in ((not_start, ring_pos - 1), (not_end, ring_pos + 1)):
+            role = jnp.where((r >= 0) & (r < half_n // 2), 2, 3)
+            pl.when(there)(functools.partial(signal, barrier, r * QUAD + role, gz))
+
+    def start_quad():
+        pl.when(soon)(functools.partial(hear, 0, QUAD - 1))
+
+        @pl.when(later & core_zero)
+        def _():
+            pl.semaphore_wait(barrier, QUAD - 1)
+            signal(news_sem.at[0], theta + 1, gz)
+
+        @pl.when((soon & (quad_pos != 0)) | (later & jnp.logical_not(core_zero)))
+        def _():
+            pl.semaphore_wait(news_sem.at[0], 1)
+
+        for i in (1, 2, 0):
+            quad_copies[i].start()
+
+        @pl.when(quad_pos == 1)
+        def _():
+            for step in range(half_n):
+                signal(barrier, other_ring(step) * QUAD + 1, gz)
+
+        pl.when(soon & (quad_pos == 2))(greet_near)
+
+        @pl.when(quad_pos == 3)
+        def _():
+            pl.when(later)(greet_near)
+            for step in range(1, half_n):
+                signal(barrier, same_ring(step) * QUAD + 3, gz)
+
+    upper = quad_pos >= QUAD // 2
+    pl.when(upper)(start_quad)
 
     loads[1].wait()
 
@@ -174,48 +225,7 @@
 
     lax.fori_loop(0, depth, to_primitive, 0)
 
-    for item in loads[2:]:
-        item.wait()
-
-    @pl.when((early & (quad_pos != 0)) | (late & jnp.logical_not(core_zero)))
-    def _():
-        pl.semaphore_wait(news_sem.at[0], 1)
-
-    def remote(src, dst, send, recv, t, g):
-        return pltpu.make_async_remote_copy(
-            src_ref=src, dst_ref=dst, send_sem=send, recv_sem=recv,
-            device_id={"theta": t, "gz": g}, device_id_type=MESH,
-        )
-
-    quad_copies = []
-    for step in range(1, QUAD):
-        copy = remote(
-            quad_v.at[quad_pos], quad_v.at[quad_pos], quad_send.at[step], quad_recv.at[step],
-            ring_pos * QUAD + (quad_pos + step) % QUAD, gz,
-        )
-        copy.start()
-        quad_copies.append(copy)
-
-    gz_next, gz_back = (gz + 1) % gz_n, (gz + gz_n - 1) % gz_n
-
-    def greet_near():
-        signal(barrier, theta, gz_next)
-        signal(barrier, theta, gz_back)
-        pl.when(not_start)(functools.partial(signal, barrier, theta - QUAD, gz))
-        pl.when(not_end)(functools.partial(signal, barrier, theta + QUAD, gz))
-
-    @pl.when(quad_pos == 1)
-    def _():
-        for step in range(half_n):
-            signal(barrier, other_ring(step) * QUAD + 1, gz)
-        pl.when(late)(greet_near)
-
-    pl.when(early & (quad_pos == 2))(greet_near)
-
-    @pl.when(quad_pos == 3)
-    def _():
-        for step in range(1, half_n):
-            signal(barrier, same_ring(step) * QUAD + 3, gz)
+    pl.when(jnp.logical_not(upper))(start_quad)
 
     radius = lane.astype(F32) + 0.5
     inv_radius = 1.0 / radius
@@ -260,6 +270,7 @@
     flip = (row == 1) | (row == 2) | (row == 5) | (row == 6)
     edge_v[...] = jnp.where(flip, -turned_v[0:8, :], turned_v[0:8, :])
 
+    loads[2].wait()
     depth_of = [levels_s[b, 0] + levels_s[b, 1] + levels_s[b, 2] + levels_s[b, 3] for b in range(2)]
     level = jnp.where(lane_block == 0, depth_of[0], depth_of[1])
     coarse = 0.5 * jnp.where(
@@ -290,12 +301,12 @@
         halo_send.at[4], halo_recv.at[4], (theta + theta_n - 1) % theta_n, gz,
     )
 
-    ahead_waits = theta == theta_n // 2 - 1
-    back_waits = theta == 0
+    ahead_far = (theta + 1) % (theta_n // 2) == 0
+    back_far = theta % (theta_n // 2) == 0
 
     def send_halos():
-        pl.when(jnp.logical_not(ahead_waits))(ahead.start)
-        pl.when(jnp.logical_not(back_waits))(back.start)
+        pl.when(jnp.logical_not(ahead_far))(ahead.start)
+        pl.when(jnp.logical_not(back_far))(back.start)
         pl.when(not_last)(up.start)
         pl.when(not_first)(down.start)
 
@@ -313,31 +324,42 @@
             prim_v[f, pl.ds(rows + 2 * width, width), :] = plane
             prim_v[f, pl.ds(rows + 3 * width, width), :] = plane
 
-    @pl.when(early)
+    @pl.when(soon)
     def _():
         hear(2, 2 + ring_near)
         heed(2)
         send_halos()
 
-    pl.when(late)(functools.partial(hear, 1, half_n + 2 + ring_near))
-
-    for copy in quad_copies:
-        copy.wait()
-
-    def spread(slot, totals):
-        index = ring_pos * (QUAD * 8) + slot
-        live = slot % 8 < count_s[ring_pos * QUAD + slot // 8]
-        code = jnp.where(live, owner_s[index] * 2 + block_s[index], -1)
-        relative = code - 2 * quad_pos - lane_block
-        value = quad_v[slot // 8, pl.ds(pl.multiple_of(slot % 8 * 8, 8), 8), :]
-        return tuple(
-            total + jnp.where(relative == 2 * QUAD * k, value, 0.0)
-            for k, total in enumerate(totals)
+    pl.when(late)(functools.partial(hear, 1, half_n))
+
+    for item in loads[3:]:
+        item.wait()
+
+    def spread(base, step, totals):
+        device, k = base + step // 4, step % 4
+        both = quad_v[device, pl.ds(pl.multiple_of(k * 8, 8), 8), :]
+        values = (
+            jnp.where(lane_block == 0, both, pltpu.roll(both, BT, 1)),
+            jnp.where(lane_block == 1, both, pltpu.roll(both, 128 - BT, 1)),
         )
-
-    totals = lax.fori_loop(
-        0, QUAD * 8, spread, tuple(jnp.zeros((8, 128), F32) for _ in range(ring_n))
-    )
+        for slot, value in zip((k, k + 4), values):
+            index = (ring_pos * QUAD + device) * 8 + slot
+            live = slot < count_s[ring_pos * QUAD + device]
+            code = jnp.where(live, owner_s[index] * 2 + block_s[index], -1)
+            relative = code - 2 * quad_pos - lane_block
+            totals = tuple(
+                total + jnp.where(relative == 2 * QUAD * z, value, 0.0)
+                for z, total in enumerate(totals)
+            )
+        return totals
+
+    totals = tuple(jnp.zeros((8, 128), F32) for _ in range(ring_n))
+    own = quad_pos // 2 * 2
+    quad_copies[0].wait()
+    totals = lax.fori_loop(0, 8, functools.partial(spread, own), totals)
+    quad_copies[1].wait()
+    quad_copies[2].wait()
+    totals = lax.fori_loop(0, 8, functools.partial(spread, 2 - own), totals)
     for k in range(ring_n):
         out_v[k] = totals[k]
 
@@ -351,26 +373,32 @@
     other_copies = [ring_copy(other_ring(step), half_n + step) for step in range(half_n)]
 
     def send_same():
-        heed(3)
         for copy in same_copies:
             copy.start()
 
     def send_other():
         heed(1)
+        pl.when(ahead_far)(ahead.start)
+        across.start()
         for copy in other_copies:
             copy.start()
-        across.start()
+        pl.when(back_far)(back.start)
 
     @pl.when(early)
     def _():
-        hear(3, half_n - 1)
+        hear(3, half_n - 1 + jnp.where(soon, 0, 2 + ring_near))
+        heed(3)
         send_same()
+        pl.when(later)(send_halos)
+        hear(1, half_n)
+        send_other()
 
     @pl.when(late)
     def _():
         send_other()
+        hear(3, half_n - 1 + 2 + ring_near)
+        heed(3)
         send_halos()
-        hear(3, half_n - 1)
         send_same()
 
     def sweep(load_plane, faces, normal, emit):
@@ -422,14 +450,6 @@
 
         sweep(axial_plane, depth + 1, 2, axial_emit)
 
-    @pl.when(early)
-    def _():
-        hear(1, half_n)
-        send_other()
-        pl.when(ahead_waits)(ahead.start)
-        pl.when(back_waits)(back.start)
-
-    ahead.wait_recv()
     back.wait_recv()
 
     def theta_plane(k):
@@ -440,7 +460,9 @@
             at = pl.ds(k, depth, stride=width)
             res_ref[f, at, :] = res_ref[f, at, :] - turn * change[f]
 
-    sweep(theta_plane, width + 1, 1, theta_emit)
+    sweep(lambda k: theta_plane(k + 2), width - 1, 1, lambda k, change: theta_emit(k + 2, change))
+    ahead.wait_recv()
+    sweep(theta_plane, 3, 1, theta_emit)
 
     ahead.wait_send()
     back.wait_send()
@@ -486,7 +508,7 @@
                 res_ref[f, at, :] = res_ref[f, at, :] + jnp.where(hits[half], moved, 0.0)
         return 0
 
-    lax.fori_loop(0, depth, correct, 0, unroll=2)
+    lax.fori_loop(0, depth, correct, 0, unroll=True)
 
 
 def copy_out(*refs):
@@ -528,7 +550,7 @@
             pltpu.VMEM((rows, 128), F32),
             pltpu.VMEM((128, rows), F32),
             pltpu.VMEM((rows, 128), F32),
-            pltpu.VMEM((QUAD, slots * fields, 128), F32),
+            pltpu.VMEM((QUAD, slots * fields // 2, 128), F32),
             pltpu.VMEM((ring_n, 8, 128), F32),
             pltpu.VMEM((ring_n, 8, 128), F32),
             pltpu.SMEM((2, 4), jnp.int32),

time: 29.8 us -> 27.8 us (0.933)
  the two profiles are of different devices: /device:TPU:472 before, /device:TPU:4 now
where the time goes in v5:
time: 27.8 us; the launch traced here: 27.7 us
  Pallas kernels  27 us (97%)
  between operations  0.64 us (2%)
    pallas_call x1, Pallas kernels, body(): pl.pallas_call(functools.partial(kernel, sizes), out_shape=(jax.ShapeDtyp...  26.2 us
    pallas_call x1, Pallas kernels, body(): pl.pallas_call(copy_out, out_shape=tuple((jax.ShapeDtypeStruct(v.shape, F...  0.83 us

profile of v5, /device:TPU:4, one launch (start us, length us, event | category | flops | bytes accessed | tf_op | source)
XLA Modules:
  0.0 27.7 jit_solution(9868802178496613811)
XLA Ops:
  0.6 26.2 %shard_map.85 = (f32[8,128,128]{2,1,0:T(8,128)S(1)}, f32[64,16]{1,0:T(8,128)S(1)}, f32[64,16]{1,0:T(8,128)S(1)}) custom-call(f32[8,128,128]{2,1,0:T(8,128)} %bitcast.6, f32[128,128]{1,0:T(8,128)} %bitcast.7, s32[2,4]{1,0:T(2,128)} %bitcast.8, s32[512]{0:T(512)} %owner_hbm.1, s32[512]{0:T(512)} %block_hbm.1, s32[64]{0:T(128)} %count_hbm.1), custom_call_target="tpu_custom_call" | custom-call | tf_op jit(solution)/shard_map/pallas_call | solution.py:534
  26.8 0.8 %shard_map.86 = (f32[8,128,128]{2,1,0:T(8,128)}, f32[64,16]{1,0:T(8,128)}, f32[64,16]{1,0:T(8,128)}) custom-call(f32[8,128,128]{2,1,0:T(8,128)S(1)} %get-tuple-element.9.refs_0_, f32[64,16]{1,0:T(8,128)S(1)} %get-tuple-element.10.refs_1_, f32[64,16]{1,0:T(8,128)S(1)} %get-tuple-element.11.refs_2_), custom_call_target="tpu_custom_call" | custom-call | tf_op jit(solution)/shard_map/pallas_call | solution.py:586

commit v6 on v5

--- a/solution.py
+++ b/solution.py
@@ -370,7 +370,10 @@
         )
 
     same_copies = [ring_copy(same_ring(step), step) for step in range(1, half_n)]
-    other_copies = [ring_copy(other_ring(step), half_n + step) for step in range(half_n)]
+    other_copies = [
+        ring_copy(half_n - half_at + p, half_n + (p + half_n - ring_pos + half_at) % half_n)
+        for p in range(half_n)
+    ]
 
     def send_same():
         for copy in same_copies:
@@ -461,11 +464,6 @@
             res_ref[f, at, :] = res_ref[f, at, :] - turn * change[f]
 
     sweep(lambda k: theta_plane(k + 2), width - 1, 1, lambda k, change: theta_emit(k + 2, change))
-    ahead.wait_recv()
-    sweep(theta_plane, 3, 1, theta_emit)
-
-    ahead.wait_send()
-    back.wait_send()
 
     across.wait()
     cell = [turned_v[f : f + 1, :] for f in range(8)]
@@ -474,7 +472,18 @@
         + half_slope(cell[f] - edge_in[f : f + 1, :], turned_v[8 + f : 9 + f, :])
         for f in range(8)
     ]
-    face_one = double_flux(left, [turned_v[16 + f : 17 + f, :] for f in range(8)], 0)
+    face_one = jnp.concatenate(
+        double_flux(left, [turned_v[16 + f : 17 + f, :] for f in range(8)], 0), axis=0
+    )
+    packed_v[...] = jnp.zeros_like(packed_v)
+    packed_v[pl.ds(0, 8, stride=4), :] = -face_one
+    packed_v[pl.ds(1, 8, stride=4), :] = face_one * (1.0 / 3.0)
+    for z in range(depth):
+        shift = (128 - z * width) % 128
+        inner = 0.5 * face_one
+        inner_ref[pl.ds(z, 8, stride=depth), :] = (
+            pltpu.roll(inner, shift, 1) if shift else inner
+        )[:, :width]
 
     for copy in same_copies + other_copies:
         copy.wait()
@@ -482,20 +491,21 @@
     for step in range(1, ring_n):
         registers = registers + in_v[(ring_pos + step) % ring_n]
     mismatch = registers - coarse
-    inner = jnp.concatenate([0.5 * v for v in face_one], axis=0)
     for z in range(depth):
         shift = (128 - z * width) % 128
         at = pl.ds(z, 8, stride=depth)
         mis_ref[at, :] = (pltpu.roll(mismatch, shift, 1) if shift else mismatch)[:, :width]
-        inner_ref[at, :] = (pltpu.roll(inner, shift, 1) if shift else inner)[:, :width]
     face = (BR * level).astype(F32)
     added = mismatch * (face / (face + 0.5))
-    nothing = jnp.zeros((1, 128), F32)
-    inner_part, outer_part = [], []
-    for f in range(8):
-        inner_part += [-face_one[f], face_one[f] * (1.0 / 3.0), nothing, nothing]
-        outer_part += [added[f : f + 1], nothing, nothing, nothing]
-    corr_v[...] = jnp.concatenate(inner_part + outer_part * 3, axis=0).T
+    for place in (BR, 2 * BR, 3 * BR):
+        packed_v[pl.ds(place, 8, stride=4), :] = added
+    corr_v[...] = packed_v[...].T
+
+    ahead.wait_recv()
+    sweep(theta_plane, 3, 1, theta_emit)
+
+    ahead.wait_send()
+    back.wait_send()
 
     hits = [(lane < 2) | (lane == BR * depth_of[half]) for half in range(2)]
 

time: 27.8 us -> 27.6 us (level)
  the two profiles are of different devices: /device:TPU:4 before, /device:TPU:1 now
where the time goes in v6:
time: 27.6 us; the launch traced here: 27.2 us
  Pallas kernels  26.6 us (96%)
  between operations  0.64 us (2%)
    pallas_call x1, Pallas kernels, body(): pl.pallas_call(functools.partial(kernel, sizes), out_shape=(jax.ShapeDtyp...  25.8 us
    pallas_call x1, Pallas kernels, body(): pl.pallas_call(copy_out, out_shape=tuple((jax.ShapeDtypeStruct(v.shape, F...  0.83 us

profile of v6, /device:TPU:1, one launch (start us, length us, event | category | flops | bytes accessed | tf_op | source)
XLA Modules:
  0.0 27.2 jit_solution(3432272073733432941)
XLA Ops:
  0.6 25.8 %shard_map.85 = (f32[8,128,128]{2,1,0:T(8,128)S(1)}, f32[64,16]{1,0:T(8,128)S(1)}, f32[64,16]{1,0:T(8,128)S(1)}) custom-call(f32[8,128,128]{2,1,0:T(8,128)} %bitcast.6, f32[128,128]{1,0:T(8,128)} %bitcast.7, s32[2,4]{1,0:T(2,128)} %bitcast.8, s32[512]{0:T(512)} %owner_hbm.1, s32[512]{0:T(512)} %block_hbm.1, s32[64]{0:T(128)} %count_hbm.1), custom_call_target="tpu_custom_call" | custom-call | tf_op jit(solution)/shard_map/pallas_call | solution.py:544
  26.4 0.8 %shard_map.86 = (f32[8,128,128]{2,1,0:T(8,128)}, f32[64,16]{1,0:T(8,128)}, f32[64,16]{1,0:T(8,128)}) custom-call(f32[8,128,128]{2,1,0:T(8,128)S(1)} %get-tuple-element.9.refs_0_, f32[64,16]{1,0:T(8,128)S(1)} %get-tuple-element.10.refs_1_, f32[64,16]{1,0:T(8,128)S(1)} %get-tuple-element.11.refs_2_), custom_call_target="tpu_custom_call" | custom-call | tf_op jit(solution)/shard_map/pallas_call | solution.py:596

commit v7 on v6

--- a/solution.py
+++ b/solution.py
@@ -186,12 +186,17 @@
 
         @pl.when(later & core_zero)
         def _():
-            pl.semaphore_wait(barrier, QUAD - 1)
+            wraps = (ring_pos == ring_n - 1) & (quad_pos == 2)
+            pl.semaphore_wait(barrier, QUAD - 1 + wraps.astype(jnp.int32))
             signal(news_sem.at[0], theta + 1, gz)
 
         @pl.when((soon & (quad_pos != 0)) | (later & jnp.logical_not(core_zero)))
         def _():
             pl.semaphore_wait(news_sem.at[0], 1)
+
+        @pl.when((ring_pos == 0) & (quad_pos == 2))
+        def _():
+            signal(barrier, (ring_n - 1) * QUAD + 2, gz)
 
         for i in (1, 2, 0):
             quad_copies[i].start()
@@ -225,7 +230,12 @@
 
     lax.fori_loop(0, depth, to_primitive, 0)
 
-    pl.when(jnp.logical_not(upper))(start_quad)
+    ahead = remote(
+        cross_v.at[:, pl.ds(rows, 2 * depth)], cross_v.at[:, pl.ds(0, 2 * depth)],
+        halo_send.at[3], halo_recv.at[3], (theta + 1) % theta_n, gz,
+    )
+    at_end = theta == theta_n - 1
+    pl.when(at_end)(ahead.start)
 
     radius = lane.astype(F32) + 0.5
     inv_radius = 1.0 / radius
@@ -264,7 +274,9 @@
             packed_v[pl.ds(at, 8), :] = packed
         return 0
 
-    lax.fori_loop(0, depth, radial, 0)
+    lax.fori_loop(0, depth // 2, radial, 0)
+    pl.when(jnp.logical_not(upper))(start_quad)
+    lax.fori_loop(depth // 2, depth, radial, 0)
     turned_v[...] = packed_v[...].T
     row = lax.broadcasted_iota(jnp.int32, (8, 128), 0)
     flip = (row == 1) | (row == 2) | (row == 5) | (row == 6)
@@ -292,10 +304,6 @@
         halo_send.at[2], halo_recv.at[2], theta, (gz + gz_n - 1) % gz_n,
     )
     not_last, not_first = gz < gz_n - 1, gz > 0
-    ahead = remote(
-        cross_v.at[:, pl.ds(rows, two_t)], cross_v.at[:, pl.ds(0, two_t)],
-        halo_send.at[3], halo_recv.at[3], (theta + 1) % theta_n, gz,
-    )
     back = remote(
         cross_v.at[:, pl.ds(two_t, two_t)], cross_v.at[:, pl.ds(rows + two_t, two_t)],
         halo_send.at[4], halo_recv.at[4], (theta + theta_n - 1) % theta_n, gz,
@@ -381,7 +389,7 @@
 
     def send_other():
         heed(1)
-        pl.when(ahead_far)(ahead.start)
+        pl.when(ahead_far & jnp.logical_not(at_end))(ahead.start)
         across.start()
         for copy in other_copies:
             copy.start()

time: 27.6 us -> 26.1 us (0.946)
  Pallas kernels: 26.6 us -> 25.3 us
    pallas_call x1, Pallas kernels: 25.8 us -> 24.5 us  [body(): pl.pallas_call(functools.partial(kernel, sizes), out_shape=(jax.ShapeDtyp...]
where the time goes in v7:
time: 26.1 us; the launch traced here: 25.9 us
  Pallas kernels  25.3 us (97%)
  between operations  0.64 us (2%)
    pallas_call x1, Pallas kernels, body(): pl.pallas_call(functools.partial(kernel, sizes), out_shape=(jax.ShapeDtyp...  24.5 us
    pallas_call x1, Pallas kernels, body(): pl.pallas_call(copy_out, out_shape=tuple((jax.ShapeDtypeStruct(v.shape, F...  0.83 us

profile of v7, /device:TPU:1, one launch (start us, length us, event | category | flops | bytes accessed | tf_op | source)
XLA Modules:
  0.0 25.9 jit_solution(12934266351936222012)
XLA Ops:
  0.6 24.5 %shard_map.85 = (f32[8,128,128]{2,1,0:T(8,128)S(1)}, f32[64,16]{1,0:T(8,128)S(1)}, f32[64,16]{1,0:T(8,128)S(1)}) custom-call(f32[8,128,128]{2,1,0:T(8,128)} %bitcast.6, f32[128,128]{1,0:T(8,128)} %bitcast.7, s32[2,4]{1,0:T(2,128)} %bitcast.8, s32[512]{0:T(512)} %owner_hbm.1, s32[512]{0:T(512)} %block_hbm.1, s32[64]{0:T(128)} %count_hbm.1), custom_call_target="tpu_custom_call" | custom-call | tf_op jit(solution)/shard_map/pallas_call | solution.py:552
  25.1 0.8 %shard_map.86 = (f32[8,128,128]{2,1,0:T(8,128)}, f32[64,16]{1,0:T(8,128)}, f32[64,16]{1,0:T(8,128)}) custom-call(f32[8,128,128]{2,1,0:T(8,128)S(1)} %get-tuple-element.9.refs_0_, f32[64,16]{1,0:T(8,128)S(1)} %get-tuple-element.10.refs_1_, f32[64,16]{1,0:T(8,128)S(1)} %get-tuple-element.11.refs_2_), custom_call_target="tpu_custom_call" | custom-call | tf_op jit(solution)/shard_map/pallas_call | solution.py:604
